TPU v7x, 32 devices: a whole 2x2x4 slice. The times are simulated.
32 devices in a mesh: row: 4 (over y, core), col: 8 (over z, x).
Axes of the slice: x: 2, y: 2, z: 4, core: 2. Of those that a mesh axis runs over, the one named last changes fastest.
Arguments:
- spectra: float32 [2, 16, 1024, 512], P(None, None, ('col', 'row')), as said below
- pair_mask: int32 [4, 8], P('row', 'col'), may hold values 0 or 1
- band_range: int32 [2], replicated, may hold values from 0 to 512, as said below
Outputs:
- correlations: bfloat16 [1024, 1024, 201], P('row', 'col')
Inputs may be any that keep to these rules, and one draw needn't show every extreme that they name: `spectra`: every channel's spectrum carries its own amplitude. band_range[0] < band_range[1].
All inputs are finite; a program needn't handle non-finite values. No bound on the sum of `pair_mask` on one device may be relied on, other than what follows from the above.
Results may differ from a plain program's by a relative error of at most 0.0061.
Values may be sent and summed in bfloat16 or wider, within the bound.
No kernel may reach another device: no remote copies, remote signals or barrier semaphores. Data moves between devices by JAX's collectives and lax.ppermute only.
A program may use at most 320 MiB of HBM per device.

v0:
```python
import math

import jax
import jax.numpy as jnp
from jax import lax
from jax.sharding import PartitionSpec as P

W = 16
FB = 512
LAGS = 201
NFFT = 15000
F0 = 60


EPS = 1e-06


def whiten(spectra):
    power_mean = jnp.mean(spectra[0] * spectra[0] + spectra[1] * spectra[1], axis=-1, keepdims=True)
    return (spectra * lax.rsqrt(power_mean + EPS)).astype(jnp.bfloat16)


def make_table(band_range):
    freq_index = jnp.arange(FB, dtype=jnp.int32)
    lag_index = jnp.arange(LAGS, dtype=jnp.int32) - LAGS // 2
    turns = jnp.mod((F0 + freq_index)[:, None] * lag_index[None, :], NFFT)
    theta = turns.astype(jnp.float32) * (2.0 * math.pi / NFFT)
    inband = ((freq_index >= band_range[0]) & (freq_index < band_range[1])).astype(jnp.float32)[
        :, None
    ]
    return jnp.concatenate([inband * jnp.cos(theta), -inband * jnp.sin(theta)], axis=0).astype(
        jnp.bfloat16
    )


def pair_block(row_block, col_block, lag_table):
    real_part = jnp.einsum(
        "wap,wbp->abp", row_block[0], col_block[0], preferred_element_type=jnp.float32
    ) + jnp.einsum("wap,wbp->abp", row_block[1], col_block[1], preferred_element_type=jnp.float32)
    imag_part = jnp.einsum(
        "wap,wbp->abp", row_block[1], col_block[0], preferred_element_type=jnp.float32
    ) - jnp.einsum("wap,wbp->abp", row_block[0], col_block[1], preferred_element_type=jnp.float32)
    cross = jnp.stack([real_part, imag_part], axis=2).astype(jnp.bfloat16)
    height = row_block.shape[2]
    width = col_block.shape[2]
    flat = cross.reshape(height * width, 2 * FB)
    summed = jnp.dot(flat, lag_table, preferred_element_type=jnp.float32)
    return (summed * (1.0 / math.sqrt(W * FB))).astype(jnp.bfloat16).reshape(height, width, LAGS)


def body(spectra, pair_mask, band_range):
    whitened = whiten(spectra)
    col_block = lax.all_gather(whitened, "row", axis=2, tiled=True)
    block_width = col_block.shape[2]
    row_count = lax.axis_size("row")
    blocks_per_row = lax.axis_size("col") // row_count
    row_id = lax.axis_index("row")
    col_id = lax.axis_index("col")
    shard_width = whitened.shape[2]
    windows = whitened.shape[1]
    bins = whitened.shape[3]
    strided = lax.all_gather(whitened, "col", axis=2, tiled=True)
    grouped = strided.reshape(2, windows, row_count, blocks_per_row, shard_width, bins)
    moved = lax.all_to_all(grouped, "row", split_axis=2, concat_axis=4, tiled=True)
    row_block = moved.reshape(2, windows, blocks_per_row * row_count * shard_width, bins)
    lag_table = make_table(band_range)
    request = (pair_mask[0, 0] == 1) & (col_id >= row_id * blocks_per_row)
    height = row_block.shape[2]
    return lax.cond(
        request,
        lambda: pair_block(row_block, col_block, lag_table),
        lambda: jnp.zeros((height, block_width, LAGS), jnp.bfloat16),
    )


def solution(mesh):
    return jax.shard_map(
        body,
        mesh=mesh,
        in_specs=(P(None, None, ("col", "row"), None), P("row", "col"), P()),
        out_specs=P("row", "col", None),
        check_vma=False,
    )
```

profile of v0, /device:TPU:0, one launch (start us, length us, event | category | flops | bytes accessed | tf_op | source)
XLA Modules:
  0.0 639.6 jit_solution(6515462427543158156)
XLA Ops:
  6.5 0.0 all-gather.5.cloned.1.call-start
  6.5 1.7 add_reduce_fusion
  8.3 2.8 multiply_convert_fusion
  11.1 0.0 all-gather.5.cloned.1.call-update
  11.2 0.0 all-gather.3.cloned.1.call-start
  11.2 0.7 all-gather.3.cloned.1.call-update
  11.9 127.0 %all-gather.5.cloned.1.call-done = bf16[2,16,256,512]{3,2,1,0:T(8,128)(2,1)} async-done(((bf16[2,16,32,512]{3,2,1,0:T(8,128)(2,1)}), bf16[2,16,256,512]{3,2,1,0:T(8,128)(2,1)}) %all-gather.5.cloned.1.call-update) | async-done | bytes 8388624 | tf_op jit(solution)/shard_map/all_gather | solution.py:62
  138.9 9.1 %copy.19 = bf16[2,16,4,2,32,512]{5,4,3,1,0,2:T(8,128)(2,1)} copy(bf16[2,16,4,2,32,512]{5,4,3,2,1,0:T(8,128)(2,1)} %bitcast.59) | data formatting | bytes 16777216 | tf_op jit(solution)/shard_map/reshape | solution.py:63
  148.0 0.0 copy-start.1
  148.0 5.8 all-to-all-start
  154.4 0.0 copy-done.1
  154.4 0.6 fusion.22
  155.0 1.1 fusion.20
  156.1 1.1 fusion.19
  157.3 2.6 multiply_convert_fusion.2
  159.9 0.9 pad_maximum_fusion.1
  160.8 27.1 %all-gather.3.cloned.1.call-done = bf16[2,16,128,512]{3,2,1,0:T(8,128)(2,1)} async-done(((bf16[2,16,32,512]{3,2,1,0:T(8,128)(2,1)}), bf16[2,16,128,512]{3,2,1,0:T(8,128)(2,1)}) %all-gather.3.cloned.1.call-update) | async-done | bytes 4194320 | tf_op jit(solution)/shard_map/all_gather | solution.py:53
  187.9 73.7 %all-to-all-done = bf16[2,16,4,2,32,512]{5,4,3,1,0,2:T(8,128)(2,1)} async-done(((bf16[2,16,4,2,32,512]{5,4,3,1,0,2:T(8,128)(2,1)}), bf16[2,16,4,2,32,512]{5,4,3,1,0,2:T(8,128)(2,1)}, u32[]{:S(2)}, u32[]{:S(2)}) %all-to-all-start) | async-done | bytes 8388640 | tf_op jit(solution)/shard_map/all_to_all | solution.py:64
  261.6 371.2 %conditional.1 = (bf16[256,128,201]{1,0,2:T(8,128)(2,1)}) conditional(s32[]{:T(128)} %convert_element_type.30, () %tuple.11, (bf16[2,16,128,512]{3,2,1,0:T(8,128)(2,1)}, bf16[2,16,1,2,4,32,512]{6,5,3,1,0,4,2:T(8,128)(2,1)}, bf16[1024,201]{1,0:T(8,128)(2,1)}) %tuple.12), branch_computations={%region_1.2_spmd, %region_2.3_spmd} | conditional | flops 15750201344 | bytes 807036928 | solution.py:69
  261.6 7.9 %copy.20 = bf16[2,16,128,512]{2,1,3,0:T(8,128)(2,1)} copy(bf16[2,16,128,512]{3,2,1,0:T(8,128)(2,1)} %get-tuple-element.22) | data formatting | bytes 8388608 | tf_op jit(solution)/shard_map
  269.4 6.2 fusion.21
  275.7 7.9 %copy.14 = bf16[16,256,512]{1,0,2:T(8,128)(2,1)} copy(bf16[16,256,512]{2,1,0:T(8,128)(2,1)} %bitcast.57) | data formatting | bytes 8388608 | tf_op jit(solution)/shard_map/cond/branch_1_fun/squeeze | solution.py:38
  283.6 7.8 %copy.15 = bf16[16,256,512]{1,0,2:T(8,128)(2,1)} copy(bf16[16,256,512]{2,1,0:T(8,128)(2,1)} %bitcast.56) | data formatting | bytes 8388608 | tf_op jit(solution)/shard_map/cond/branch_1_fun/squeeze | solution.py:39
  291.4 26.3 %fusion.11 = f32[512,128,256]{2,1,0:T(8,128)} fusion(bf16[16,256,512]{1,0,2:T(8,128)(2,1)} %copy.15, bf16[2,16,128,512]{2,1,3,0:T(8,128)(2,1)} %copy.20), kind=kOutput, calls=%fused_computation.13 | convolution fusion | flops 536870912 | bytes 73400320 | tf_op jit(solution)/shard_map/cond/branch_1_fun/wap,wbp->abp/dot_general | solution.py:40
  317.7 36.4 %fusion.10 = bf16[256,128,1,512]{0,1,3,2:T(8,128)(2,1)} fusion(f32[512,128,256]{2,1,0:T(8,128)} %fusion.11, bf16[16,256,512]{1,0,2:T(8,128)(2,1)} %copy.14, bf16[2,16,128,512]{2,1,3,0:T(8,128)(2,1)} %copy.20), kind=kOutput, calls=%fused_computation.9 | convolution fusion | flops 570425344 | bytes 106954752 | tf_op jit(solution)/shard_map/cond/branch_1_fun/wap,wbp->abp/dot_general | solution.py:42
  354.1 26.3 %fusion.12 = f32[512,128,256]{2,1,0:T(8,128)} fusion(bf16[16,256,512]{1,0,2:T(8,128)(2,1)} %copy.14, bf16[2,16,128,512]{2,1,3,0:T(8,128)(2,1)} %copy.20), kind=kOutput, calls=%fused_computation.14 | convolution fusion | flops 536870912 | bytes 73400320 | tf_op jit(solution)/shard_map/cond/branch_1_fun/wap,wbp->abp/dot_general | solution.py:37
  380.4 36.3 %fusion.9 = bf16[256,128,1,512]{0,1,3,2:T(8,128)(2,1)} fusion(f32[512,128,256]{2,1,0:T(8,128)} %fusion.12, bf16[16,256,512]{1,0,2:T(8,128)(2,1)} %copy.15, bf16[2,16,128,512]{2,1,3,0:T(8,128)(2,1)} %copy.20), kind=kOutput, calls=%fused_computation.8 | convolution fusion | flops 570425344 | bytes 106954752 | tf_op jit(solution)/shard_map/cond/branch_1_fun/wap,wbp->abp/dot_general | solution.py:39
  416.7 44.6 %pad_maximum_fusion = bf16[256,128,2,512]{0,1,3,2:T(8,128)(2,1)} fusion(bf16[256,128,1,512]{0,1,3,2:T(8,128)(2,1)} %fusion.10, bf16[256,128,1,512]{0,1,3,2:T(8,128)(2,1)} %fusion.9), kind=kLoop, calls=%fused_computation.3 | loop fusion | flops 33554432 | bytes 134217728 | tf_op jit(solution)/shard_map/cond/branch_1_fun/stack | solution.py:43
  461.3 0.0 copy-start
  461.3 81.5 %copy.18 = bf16[256,128,2,512]{1,0,3,2:T(8,128)(2,1)} copy(bf16[256,128,2,512]{0,1,3,2:T(8,128)(2,1)} %pad_maximum_fusion) | data formatting | bytes 134217728 | tf_op jit(solution)/shard_map/cond/branch_1_fun/stack | solution.py:43
  542.8 0.0 copy-done
  542.8 75.7 %fusion.6 = bf16[32768,201]{0,1:T(8,128)(2,1)} fusion(bf16[1024,201]{1,0:T(8,128)(2,1)S(1)} %copy-done, bf16[128,8,256,128]{3,2,1,0:T(8,128)(2,1)} %bitcast.19), kind=kOutput, calls=%fused_computation.7 | convolution fusion | flops 13502054400 | bytes 80693248 | tf_op jit(solution)/shard_map/cond/branch_1_fun/dot_general | solution.py:47
  618.5 8.4 %copy.23 = bf16[26,8,256,128]{3,2,1,0:T(8,128)(2,1)S(1)} copy(bf16[26,8,256,128]{3,1,2,0:T(8,128)(2,1)} %bitcast.58) | data formatting | bytes 27262976 | tf_op jit(solution)/shard_map/cond
  626.8 6.0 slice_bitcast_fusion
  (3 shorter events, 0.0 us)
Async XLA Ops:
  6.5 132.4 %all-gather.5.cloned.1.call-start = ((), (), s32[]{:S(2)}) async-start(), calls=%async_computation.2 | async-start | bytes 9437184 | tf_op jit(solution)/shard_map/all_gather | solution.py:62
  11.2 176.7 %all-gather.3.cloned.1.call-start = ((), (), s32[]{:S(2)}) async-start(), calls=%async_computation.1 | async-start | bytes 5242880 | tf_op jit(solution)/shard_map/all_gather | solution.py:53
  148.0 6.4 %copy-start.1 = (s32[2]{0:T(128)S(1)}, s32[2]{0:T(128)}, u32[]{:S(2)}) copy-start(s32[2]{0:T(128)} %param.7) | copy-start | bytes 28
  148.0 113.6 %all-to-all-start = ((bf16[2,16,4,2,32,512]{5,4,3,1,0,2:T(8,128)(2,1)}), bf16[2,16,4,2,32,512]{5,4,3,1,0,2:T(8,128)(2,1)}, u32[]{:S(2)}, u32[]{:S(2)}) async-start(bf16[2,16,4,2,32,512]{5,4,3,1,0,2:T(8,128)(2,1)} %copy.19), calls=%async_computation | async-start | bytes 16777216 | tf_op jit(solution)/shard_map/all_to_all | solution.py:64
  461.3 81.5 %copy-start = (bf16[1024,201]{1,0:T(8,128)(2,1)S(1)}, bf16[1024,201]{1,0:T(8,128)(2,1)}, u32[]{:S(2)}) copy-start(bf16[1024,201]{1,0:T(8,128)(2,1)} %get-tuple-element.17) | copy-start | bytes 1234948 | tf_op jit(solution)/shard_map/cond
Sparse Core Ops, SparseCore 0:
  11.3 127.5 all-gather.4
  140.5 47.3 all-gather.2
where the time goes:
time: 643 us; the launch traced here: 640 us
  waiting for transfers between devices  229 us (36%)
  matrix products  201 us (31%)
  local copies, waits for them, and re-layouts  135 us (21%)
  other arithmetic  55 us (9%)
  between operations  14.1 us (2%)
    all_gather x1, waiting for transfers between devices, body(): strided = lax.all_gather(whitened, 'col', axis=2, tiled=True)  127 us
    another operation x1, local copies, waits for them, and re-layouts, pair_block(): cross = jnp.stack([real_part, imag_part], axis=2).astype(jnp.bfloat16)  81.5 us
    dot_general x1, matrix products, pair_block(): summed = jnp.dot(flat, lag_table, preferred_element_type=jnp.float32)  75.7 us
    all_to_all x1, waiting for transfers between devices, body(): lax.all_to_all(grouped, 'row', split_axis=2, concat_axis=4, tiled=True)  73.7 us
    another operation x1, other arithmetic, pair_block(): cross = jnp.stack([real_part, imag_part], axis=2).astype(jnp.bfloat16)  44.6 us
    dot_general x1, matrix products, pair_block(): jnp.einsum('wap,wbp->abp', row_block[0], col_block[1], preferred_element_...  36.4 us
    dot_general x1, matrix products, pair_block(): jnp.einsum('wap,wbp->abp', row_block[1], col_block[1], preferred_element_...  36.3 us
    all_gather x1, waiting for transfers between devices, body(): col_block = lax.all_gather(whitened, 'row', axis=2, tiled=True)  27.1 us
  transfers between devices with their start and end apart: 3, of which 3 were waited for; matrix products, arithmetic and copies ran while one was open for 2% of the time, Pallas kernels for 0%

commit v1 on v0

v1 whole, which is shorter than its diff:
```python
import functools
import math

import jax
import jax.numpy as jnp
from jax import lax
from jax.experimental import pallas as pl
from jax.experimental.pallas import tpu as pltpu
from jax.sharding import PartitionSpec as P

W = 16
FB = 512
LAGS = 201
NFFT = 15000
F0 = 60
EPS = 1e-06

SEGMENTS = 4
ROWS = FB // SEGMENTS
PAIRS = ROWS // 2
LAG_PAD = 208


def whiten_kernel(*refs, width, parts):
    x_refs, out_refs, scratch = refs[:SEGMENTS], refs[SEGMENTS : SEGMENTS + parts], refs[-1]

    def channel(c, carry):
        tiles = [x_ref[pl.ds(c, 2 * W, stride=width), :] for x_ref in x_refs]
        total = sum(v[:W] * v[:W] + v[W:] * v[W:] for v in tiles)
        power = jnp.sum(total, axis=-1, keepdims=True) * (1.0 / FB)
        scale = lax.rsqrt(power + EPS)
        scale = jnp.concatenate([scale, scale], axis=0)
        stacked = jnp.concatenate([v * scale for v in tiles], axis=0)
        scratch[pl.ds(c, ROWS, stride=width), :] = stacked.T
        return carry

    lax.fori_loop(0, width, channel, 0, unroll=2)
    step = width // parts
    full = scratch[...].reshape(ROWS, width, 128).astype(jnp.bfloat16)
    for g in range(parts):
        out_refs[g][...] = full[:, g * step : (g + 1) * step, :]


def whiten(spectra, parts):
    width = spectra.shape[2]
    step = width // parts
    lines = 2 * W * width
    flat = spectra.reshape(lines, FB)
    return pl.pallas_call(
        functools.partial(whiten_kernel, width=width, parts=parts),
        out_shape=[jax.ShapeDtypeStruct((ROWS, step, 128), jnp.bfloat16)] * parts,
        grid=(1,),
        in_specs=[pl.BlockSpec((lines, ROWS), functools.partial(lambda q, i: (0, q), q)) for q in range(SEGMENTS)],
        out_specs=[pl.BlockSpec((ROWS, step, 128), lambda i: (0, 0, 0))] * parts,
        scratch_shapes=[pltpu.VMEM((ROWS * width, 128), jnp.float32)],
        compiler_params=pltpu.CompilerParams(vmem_limit_bytes=40 << 20),
        name="whiten",
    )(*[flat] * SEGMENTS)


def weights_kernel(offset_ref, *refs, count, step):
    in_refs, out_ref, scratch = refs[:count], refs[count], refs[count + 1]
    for i in range(count):
        at = pl.multiple_of(offset_ref[i], step)
        scratch[:, pl.ds(at, step), :] = in_refs[i][...].astype(jnp.float32)

    def row(t, carry):
        for s in range(2):
            real = scratch[2 * t + s].T
            pieces = []
            for q in range(SEGMENTS):
                lo = q * 2 * W
                pieces += [-real[lo + W : lo + 2 * W], real[lo : lo + W]]
            imag = jnp.concatenate(pieces, axis=0)
            both = jnp.concatenate([real, imag], axis=1).astype(jnp.bfloat16)
            out_ref[t, s * 128 : (s + 1) * 128, :] = both
        return carry

    lax.fori_loop(0, out_ref.shape[0], row, 0, unroll=2)


def weights(offsets, shards):
    count = len(shards)
    step = shards[0].shape[1]
    tiles = 4
    return pl.pallas_call(
        functools.partial(weights_kernel, count=count, step=step),
        out_shape=jax.ShapeDtypeStruct((PAIRS, 256, 256), jnp.bfloat16),
        grid_spec=pltpu.PrefetchScalarGridSpec(
            num_scalar_prefetch=1,
            grid=(tiles,),
            in_specs=[pl.BlockSpec((ROWS // tiles, step, 128), lambda i, o: (i, 0, 0))] * count,
            out_specs=pl.BlockSpec((PAIRS // tiles, 256, 256), lambda i, o: (i, 0, 0)),
            scratch_shapes=[pltpu.VMEM((ROWS // tiles, count * step, 128), jnp.float32)],
        ),
        compiler_params=pltpu.CompilerParams(vmem_limit_bytes=40 << 20),
        name="weights",
    )(offsets, *shards)


def pair_kernel(meta_ref, *refs, count, step, unroll_sum, unroll_lag):
    x_refs = refs[:count]
    w_ref, t_ref, _, out_ref = refs[count : count + 4]
    xbuf, wide, wbuf, tbuf, cross, lags, stage, sems = refs[count + 4 :]
    height = count * step

    @pl.when(meta_ref[0] == 1)
    def _():
        copies = [
            pltpu.make_async_copy(x_refs[i], xbuf.at[:, i * step : (i + 1) * step, :], sems.at[i])
            for i in range(count)
        ]
        copies.append(pltpu.make_async_copy(w_ref, wbuf, sems.at[count]))
        copies.append(pltpu.make_async_copy(t_ref, tbuf, sems.at[count + 1]))
        for copy in copies:
            copy.start()
        for copy in copies[:count]:
            copy.wait()
        wide[...] = xbuf[...].astype(jnp.float32).reshape(ROWS * height, 128)
        for copy in copies[count:]:
            copy.wait()

        sub = lax.broadcasted_iota(jnp.int32, (8, 128), 0)
        segment = lax.broadcasted_iota(jnp.int32, (8, 128), 1) // (2 * W)
        masks = (segment == sub, segment == sub - SEGMENTS)

        def window_sums(h, carry):
            halves = []
            for u in range(2):
                pair = 2 * h + u
                rows = []
                for a in range(height):
                    halves_of_k = [
                        jnp.where(masks[s], wide[pl.ds((2 * pair + s) * height + a, 8, stride=0), :], 0.0)
                        for s in range(2)
                    ]
                    rows.append(jnp.concatenate(halves_of_k, axis=1))
                left = jnp.concatenate(rows, axis=0).astype(jnp.bfloat16)
                sums = jnp.dot(left, wbuf[pair], preferred_element_type=jnp.float32)
                halves.append(sums.reshape(height, 8, 256))
            both = jnp.concatenate(halves, axis=1).astype(jnp.bfloat16)
            cross[:, pl.ds(pl.multiple_of(h * 16, 16), 16), :] = both
            return carry

        lax.fori_loop(0, PAIRS // 2, window_sums, 0, unroll=unroll_sum)

        def lag_sums(h, carry):
            first, second = cross[2 * h], cross[2 * h + 1]
            real = jnp.concatenate([first[:, :128], second[:, :128]], axis=1)
            imag = jnp.concatenate([first[:, 128:], second[:, 128:]], axis=1)
            right = jnp.concatenate([real, imag], axis=0)
            out = jnp.dot(tbuf[...], right, preferred_element_type=jnp.float32)
            out = out * (1.0 / math.sqrt(W * FB))
            lags[pl.ds(2 * h, LAG_PAD, stride=height), :] = out[:, :128]
            lags[pl.ds(2 * h + 1, LAG_PAD, stride=height), :] = out[:, 128:]
            return carry

        lax.fori_loop(0, height // 2, lag_sums, 0, unroll=unroll_lag)
        full = lags[...].reshape(LAG_PAD, height, 128)[:LAGS].astype(jnp.bfloat16)
        stage[...] = full
        backs = [
            pltpu.make_async_copy(
                stage.at[:, i * step : (i + 1) * step, :],
                out_ref.at[:, pl.ds(pl.multiple_of(meta_ref[1 + i], step), step), :],
                sems.at[i],
            )
            for i in range(count)
        ]
        for back in backs:
            back.start()
        for back in backs:
            back.wait()


def pair_block(meta, shards, right, table, out, unroll_sum=2, unroll_lag=2):
    count = len(shards)
    step = shards[0].shape[1]
    height = count * step
    anywhere = pl.BlockSpec(memory_space=pl.ANY)
    return pl.pallas_call(
        functools.partial(pair_kernel, count=count, step=step, unroll_sum=unroll_sum, unroll_lag=unroll_lag),
        out_shape=jax.ShapeDtypeStruct(out.shape, out.dtype),
        grid_spec=pltpu.PrefetchScalarGridSpec(
            num_scalar_prefetch=1,
            grid=(),
            in_specs=[anywhere] * (count + 3),
            out_specs=anywhere,
            scratch_shapes=[
                pltpu.VMEM((ROWS, height, 128), jnp.bfloat16),
                pltpu.VMEM((ROWS * height, 128), jnp.float32),
                pltpu.VMEM((PAIRS, 256, 256), jnp.bfloat16),
                pltpu.VMEM((LAG_PAD, 2 * FB), jnp.bfloat16),
                pltpu.VMEM((height, FB, 256), jnp.bfloat16),
                pltpu.VMEM((LAG_PAD * height, 128), jnp.float32),
                pltpu.VMEM((LAGS, height, 128), jnp.bfloat16),
                pltpu.SemaphoreType.DMA((count + 2,)),
            ],
        ),
        input_output_aliases={count + 3: 0},
        compiler_params=pltpu.CompilerParams(vmem_limit_bytes=60 << 20),
        cost_estimate=pl.CostEstimate(
            flops=2 * height * FB * 256 * 8 * 32 + 2 * height * 128 * 2 * FB * LAG_PAD,
            bytes_accessed=PAIRS * 256 * 256 * 2 + 2 * height * 128 * LAGS,
            transcendentals=0,
        ),
        name="pair_block",
    )(meta, *shards, right, table, out)


def make_table(band_range):
    order = jnp.arange(FB, dtype=jnp.int32)
    freq_index = (order % SEGMENTS) * ROWS + order // SEGMENTS
    lag_index = jnp.arange(LAG_PAD, dtype=jnp.int32) - LAGS // 2
    turns = jnp.mod((F0 + freq_index)[None, :] * lag_index[:, None], NFFT)
    theta = turns.astype(jnp.float32) * (2.0 * math.pi / NFFT)
    inband = ((freq_index >= band_range[0]) & (freq_index < band_range[1])).astype(jnp.float32)[None, :]
    return jnp.concatenate([inband * jnp.cos(theta), -inband * jnp.sin(theta)], axis=1).astype(jnp.bfloat16)


def bystander_body(whitened, request, table, out):
    (shard,) = whitened
    width = shard.shape[1]
    row_count = lax.axis_size("row")
    blocks_per_row = lax.axis_size("col") // row_count
    column = lax.all_gather(shard, "row", axis=1, tiled=True)
    strided = lax.all_gather(shard, "col", axis=0)
    grouped = strided.reshape(row_count, blocks_per_row, ROWS, width, 128)
    moved = lax.all_to_all(grouped, "row", split_axis=0, concat_axis=0)
    block = jnp.transpose(moved, (2, 1, 0, 3, 4)).reshape(ROWS, blocks_per_row * row_count * width, 128)
    right = weights(jnp.zeros((1,), jnp.int32), [column])
    group = min(64, block.shape[1])
    for at in range(0, block.shape[1], group):
        meta = jnp.stack([request, jnp.int32(at)])
        out = pair_block(meta, [block[:, at : at + group]], right, table, out)
    return out


def relay_body(whitened, request, table, out, row_count, blocks_per_row):
    (shard,) = whitened
    width = shard.shape[1]
    row_id = lax.axis_index("row")
    col_id = lax.axis_index("col")
    plane = col_id // blocks_per_row
    side = col_id % blocks_per_row
    depth = plane - row_id
    devices = [(r, p, x) for r in range(row_count) for p in range(row_count) for x in range(blocks_per_row)]

    def number(r, p, x):
        return (r * row_count + p) * blocks_per_row + x

    def move(value, pairs):
        return lax.ppermute(value, ("row", "col"), [(number(*a), number(*b)) for a, b in pairs])

    def core_flip(value):
        return move(value, [((r, p, x), (r ^ 1, p, x)) for r, p, x in devices])

    def chip_flip(value):
        return move(value, [((r, p, x), (r ^ 2, p, x)) for r, p, x in devices])

    across = chip_flip(shard)
    own = [shard, core_flip(shard), across, core_flip(across)]
    count = len(own)
    offsets = jnp.stack([(row_id ^ k) * width for k in range(count)])
    right = weights(offsets, own)
    came = None
    for s in range(count + row_count - 1):
        busy = [(r, p, x) for r, p, x in devices if p >= r and 0 <= s - (p - r) < count]
        if s == 0:
            front = own[0]
        elif s < count:
            front = jnp.where(depth == 0, own[s], came)
        else:
            front = came
        came = move(front, [((r, p, x), (r, p + 1, x)) for r, p, x in busy if p + 1 < row_count])
        other = move(front, [((r, p, x), (r, p, 1 - x)) for r, p, x in busy])
        k = s - depth
        valid = jnp.where((k >= 0) & (k < count), request, 0)
        source = row_id ^ jnp.clip(k, 0, count - 1)
        meta = jnp.stack(
            [valid, (side * row_count + source) * width, ((1 - side) * row_count + source) * width]
        ).astype(jnp.int32)
        out = pair_block(meta, [front, other], right, table, out, 4, 4)
    return out


def body(spectra, pair_mask, band_range):
    row_id = lax.axis_index("row")
    col_id = lax.axis_index("col")
    row_count = lax.axis_size("row")
    blocks_per_row = lax.axis_size("col") // row_count
    width = spectra.shape[2]
    whitened = whiten(spectra, 1)
    request = ((pair_mask[0, 0] == 1) & (col_id >= row_id * blocks_per_row)).astype(jnp.int32)
    table = make_table(band_range)
    out = jnp.zeros((LAGS, blocks_per_row * row_count * width, row_count * width), jnp.bfloat16)
    if row_count == 4 and blocks_per_row == 2:
        out = relay_body(whitened, request, table, out, row_count, blocks_per_row)
    else:
        out = bystander_body(whitened, request, table, out)
    return jnp.transpose(out, (1, 2, 0))


def solution(mesh):
    return jax.shard_map(
        body,
        mesh=mesh,
        in_specs=(P(None, None, ("col", "row"), None), P("row", "col"), P()),
        out_specs=P("row", "col", None),
        check_vma=False,
    )
```

time: 643 us -> 237 us (0.37)
  the two profiles are of different devices: /device:TPU:0 before, /device:TPU:26 now
where the time goes in v1:
time: 237 us; the launch traced here: 236 us
  Pallas kernels  99.5 us (42%)
  waiting for transfers between devices  81.1 us (34%)
  starting transfers between devices  24.5 us (10%)
  local copies, waits for them, and re-layouts  14.7 us (6%)
  other arithmetic  14.5 us (6%)
    pallas_call x7, Pallas kernels, pair_block(): pl.pallas_call(functools.partial(pair_kernel, count=count, step=step, unr...  86 us
    ppermute x16, waiting for transfers between devices, move(): lax.ppermute(value, ('row', 'col'), [(number(*a), number(*b)) for a, b in...  81.1 us
    ppermute x16, starting transfers between devices, move(): lax.ppermute(value, ('row', 'col'), [(number(*a), number(*b)) for a, b in...  24.5 us
    broadcast_in_dim x1, local copies, waits for them, and re-layouts, body(): jnp.zeros((LAGS, blocks_per_row * row_count * width, row_count * width),...  8.3 us
    pallas_call x1, Pallas kernels, whiten(): pl.pallas_call(functools.partial(whiten_kernel, width=width, parts=parts)...  6.96 us
    pallas_call x1, Pallas kernels, weights(): pl.pallas_call(functools.partial(weights_kernel, count=count, step=step),...  6.46 us
    unnamed x16, local copies, waits for them, and re-layouts  5.86 us
    select_n x3, other arithmetic, relay_body(): front = jnp.where(depth == 0, own[s], came)  4.85 us
  transfers between devices with their start and end apart: 16, of which 5 were waited for; matrix products, arithmetic and copies ran while one was open for 10% of the time, Pallas kernels for 30%

profile of v1, /device:TPU:26, one launch (start us, length us, event | category | flops | bytes accessed | tf_op | source)
XLA Modules:
  0.0 235.6 jit_solution(2545047282160213396)
XLA Ops:
  0.0 1.6 copy-done.1
  1.6 7.0 %whiten.1.refs_0_ = bf16[128,32,128]{2,1,0:T(8,128)(2,1)S(1)} custom-call(f32[1024,512]{1,0:T(8,128)S(1)} %bitcast.30, f32[1024,512]{1,0:T(8,128)S(1)} %bitcast.31, f32[1024,512]{1,0:T(8,128)S(1)} %bitcast.32, f32[1024,512]{1,0:T(8,128)S(1)} %bitcast.33), custom_call_target="tpu_custom_call" | custom-call | tf_op jit(solution)/shard_map/whiten/pallas_call | solution.py:49
  8.6 0.0 copy-start.2
  8.6 0.1 collective-permute-start.2
  8.7 1.7 collective-permute-start.3
  10.3 1.2 collective-permute-start
  11.6 0.0 collective-permute-done.2.refs_1_
  11.6 0.0 collective-permute-done.3
  11.6 1.3 broadcast_select_fusion.2.refs_0_
  12.9 0.0 copy-start.3
  12.9 0.7 collective-permute-start.4
  13.6 22.2 %collective-permute-done.refs_2_ = bf16[128,32,128]{2,1,0:T(8,128)(2,1)S(1)} collective-permute-done((bf16[128,32,128]{2,1,0:T(8,128)(2,1)S(1)}, bf16[128,32,128]{2,1,0:T(8,128)(2,1)S(1)}, u32[]{:S(2)}, u32[]{:S(2)}) %collective-permute-start) | collective-permute-done | bytes 1048608 | tf_op jit(solution)/shard_map/ppermute | solution.py:252
  35.9 0.0 collective-permute-start.1
  35.9 0.0 collective-permute-done.4
  35.9 1.2 broadcast_select_fusion.1.refs_0_
  37.1 0.0 copy-done.3
  37.1 1.3 collective-permute-start.5
  38.4 1.7 collective-permute-start.15
  40.8 0.6 pad_add_fusion.7.meta_ref
  41.4 0.7 pad_add_fusion.6.meta_ref
  42.0 0.6 pad_add_fusion.5.meta_ref
  42.6 0.7 pad_add_fusion.4.meta_ref
  43.3 0.6 pad_add_fusion.3.meta_ref
  43.9 0.7 pad_add_fusion.2.meta_ref
  44.5 0.0 collective-permute-done.1.refs_3_
  44.6 35.8 %collective-permute-done.5 = bf16[128,32,128]{2,1,0:T(8,128)(2,1)} collective-permute-done((bf16[128,32,128]{2,1,0:T(8,128)(2,1)}, bf16[128,32,128]{2,1,0:T(8,128)(2,1)}, u32[]{:S(2)}, u32[]{:S(2)}) %collective-permute-start.5) | collective-permute-done | bytes 1048608 | tf_op jit(solution)/shard_map/ppermute | solution.py:252
  80.3 2.3 broadcast_select_fusion.refs_0_
  82.7 1.3 collective-permute-start.6
  84.0 0.6 pad_add_fusion.meta_ref
  84.6 0.1 pad_add_fusion.1.offset_ref
  84.7 0.6 fusion.15
  85.2 1.2 and_convert_fusion
  86.5 1.2 fusion.14
  87.7 1.6 collective-permute-start.14
  89.3 2.0 multiply_convert_fusion.1
  91.3 0.8 pad_maximum_fusion.refs_3_
  92.1 1.7 collective-permute-start.13
  93.8 6.5 %weights.1.refs_2_ = bf16[64,256,256]{2,1,0:T(8,128)(2,1)S(1)} custom-call(s32[4]{0:T(128)S(1)} %pad_add_fusion.1.offset_ref, bf16[128,32,128]{2,1,0:T(8,128)(2,1)S(1)} %whiten.1.refs_0_, bf16[128,32,128]{2,1,0:T(8,128)(2,1)S(1)} %collective-permute-done.2.refs_1_, bf16[128,32,128]{2,1,0:T(8,128)(2,1)S(1)} %collective-permute-done.refs_2_, ...), custom_call_target="tpu_custom_call" | custom-call | tf_op jit(solution)/shard_map/weights/pallas_call | solution.py:86
  100.3 3.3 %copy-done = bf16[64,256,256]{2,1,0:T(8,128)(2,1)} copy-done((bf16[64,256,256]{2,1,0:T(8,128)(2,1)}, bf16[64,256,256]{2,1,0:T(8,128)(2,1)S(1)}, u32[]{:S(2)}) %copy-start) | copy-done | bytes 8388632
  103.5 6.0 %collective-permute-done.6.refs_0_ = bf16[128,32,128]{2,1,0:T(8,128)(2,1)} collective-permute-done((bf16[128,32,128]{2,1,0:T(8,128)(2,1)}, bf16[128,32,128]{2,1,0:T(8,128)(2,1)}, u32[]{:S(2)}, u32[]{:S(2)}) %collective-permute-start.6) | collective-permute-done | bytes 1048608 | tf_op jit(solution)/shard_map/ppermute | solution.py:252
  109.5 1.3 collective-permute-start.7
  110.8 0.0 collective-permute-done.15.refs_1_
  110.8 8.3 %broadcast_in_dim.2.refs_4_ = bf16[201,256,128]{2,1,0:T(8,128)(2,1)} broadcast(bf16[]{:T(256)} %constant.95.clone.1), dimensions={} | broadcast | bytes 13172738 | tf_op jit(solution)/shard_map/broadcast_in_dim | solution.py:295
  119.1 0.7 pair_block.7.refs_4_
  119.8 2.4 %collective-permute-start.12 = (bf16[128,32,128]{2,1,0:T(8,128)(2,1)}, bf16[128,32,128]{2,1,0:T(8,128)(2,1)}, u32[]{:S(2)}, u32[]{:S(2)}) collective-permute-start(bf16[128,32,128]{2,1,0:T(8,128)(2,1)} %broadcast_select_fusion.refs_0_), channel_id=1, source_target_pairs={{0,1},{1,0},{2,3},{3,2},{4,5},{5,4},{6,7},{7,6},{10,11},{11,10},{1... | collective-permute-start | bytes 3145736 | tf_op jit(solution)/shard_map/ppermute | solution.py:252
  122.3 0.0 collective-permute-done.14.refs_1_
  122.3 0.7 pair_block.8.refs_4_
  123.0 3.4 %collective-permute-start.11 = (bf16[128,32,128]{2,1,0:T(8,128)(2,1)}, bf16[128,32,128]{2,1,0:T(8,128)(2,1)S(1)}, u32[]{:S(2)}, u32[]{:S(2)}) collective-permute-start(bf16[128,32,128]{2,1,0:T(8,128)(2,1)} %collective-permute-done.6.refs_0_), channel_id=1, source_target_pairs={{2,3},{3,2},{4,5},{5,4},{6,7},{7,6},{12,13},{13,12},{14,15},{15,14... | collective-permute-start | bytes 3145736 | tf_op jit(solution)/shard_map/ppermute | solution.py:252
  126.4 8.9 %collective-permute-done.7.refs_0_ = bf16[128,32,128]{2,1,0:T(8,128)(2,1)S(1)} collective-permute-done((bf16[128,32,128]{2,1,0:T(8,128)(2,1)}, bf16[128,32,128]{2,1,0:T(8,128)(2,1)S(1)}, u32[]{:S(2)}, u32[]{:S(2)}) %collective-permute-start.7) | collective-permute-done | bytes 1048608 | tf_op jit(solution)/shard_map/ppermute | solution.py:252
  135.4 1.3 collective-permute-start.8
  136.7 0.0 collective-permute-done.13.refs_1_
  136.7 0.9 pair_block.9.refs_4_
  137.6 2.4 %collective-permute-start.10 = (bf16[128,32,128]{2,1,0:T(8,128)(2,1)S(1)}, bf16[128,32,128]{2,1,0:T(8,128)(2,1)}, u32[]{:S(2)}, u32[]{:S(2)}) collective-permute-start(bf16[128,32,128]{2,1,0:T(8,128)(2,1)S(1)} %collective-permute-done.7.refs_0_), channel_id=1, source_target_pairs={{4,5},{5,4},{6,7},{7,6},{14,15},{15,14}} | collective-permute-start | bytes 3145736 | tf_op jit(solution)/shard_map/ppermute | solution.py:252
  140.0 8.1 %collective-permute-done.12.refs_1_ = bf16[128,32,128]{2,1,0:T(8,128)(2,1)} collective-permute-done((bf16[128,32,128]{2,1,0:T(8,128)(2,1)}, bf16[128,32,128]{2,1,0:T(8,128)(2,1)}, u32[]{:S(2)}, u32[]{:S(2)}) %collective-permute-start.12) | collective-permute-done | bytes 1048608 | tf_op jit(solution)/shard_map/ppermute | solution.py:252
  148.2 20.9 %pair_block.10.refs_4_ = bf16[201,256,128]{2,1,0:T(8,128)(2,1)} custom-call(s32[3]{0:T(128)} %pad_add_fusion.4.meta_ref, bf16[128,32,128]{2,1,0:T(8,128)(2,1)} %broadcast_select_fusion.refs_0_, bf16[128,32,128]{2,1,0:T(8,128)(2,1)} %collective-permute-done.12.refs_1_, bf16[64,256,256]{2,1,0:T(8,128)(2,1)} %copy-done, ...), custom_call_target="tpu_custom_call", output_to_operand_aliasing={{}: (5, {})} | custom-call | flops 7784628224 | bytes 11681792 | tf_op jit(solution)/shard_map/pair_block/pallas_call | solution.py:180
  169.1 0.0 collective-permute-done.8.refs_0_
  169.1 2.4 %collective-permute-start.9 = (bf16[128,32,128]{2,1,0:T(8,128)(2,1)S(1)}, bf16[128,32,128]{2,1,0:T(8,128)(2,1)}, u32[]{:S(2)}, u32[]{:S(2)}) collective-permute-start(bf16[128,32,128]{2,1,0:T(8,128)(2,1)S(1)} %collective-permute-done.8.refs_0_), channel_id=1, source_target_pairs={{6,7},{7,6}} | collective-permute-start | bytes 3145736 | tf_op jit(solution)/shard_map/ppermute | solution.py:252
  171.6 0.0 collective-permute-done.11.refs_1_
  171.6 1.0 copy-done.6
  172.6 20.9 %pair_block.11.refs_4_ = bf16[201,256,128]{2,1,0:T(8,128)(2,1)} custom-call(s32[3]{0:T(128)} %pad_add_fusion.3.meta_ref, bf16[128,32,128]{2,1,0:T(8,128)(2,1)} %collective-permute-done.6.refs_0_, bf16[128,32,128]{2,1,0:T(8,128)(2,1)} %copy-done.6, bf16[64,256,256]{2,1,0:T(8,128)(2,1)} %copy-done, ...), custom_call_target="tpu_custom_call", output_to_operand_aliasing={{}: (5, {})} | custom-call | flops 7784628224 | bytes 11681792 | tf_op jit(solution)/shard_map/pair_block/pallas_call | solution.py:180
  193.5 0.0 collective-permute-done.10.refs_1_
  193.5 20.9 %pair_block.12.refs_4_ = bf16[201,256,128]{2,1,0:T(8,128)(2,1)} custom-call(s32[3]{0:T(128)} %pad_add_fusion.2.meta_ref, bf16[128,32,128]{2,1,0:T(8,128)(2,1)} %copy-done.4, bf16[128,32,128]{2,1,0:T(8,128)(2,1)} %collective-permute-done.10.refs_1_, bf16[64,256,256]{2,1,0:T(8,128)(2,1)} %copy-done, ...), custom_call_target="tpu_custom_call", output_to_operand_aliasing={{}: (5, {})} | custom-call | flops 7784628224 | bytes 11681792 | tf_op jit(solution)/shard_map/pair_block/pallas_call | solution.py:180
  214.5 0.0 collective-permute-done.9.refs_1_
  214.5 20.9 %pair_block.13 = bf16[201,256,128]{2,1,0:T(8,128)(2,1)} custom-call(s32[3]{0:T(128)} %pad_add_fusion.meta_ref, bf16[128,32,128]{2,1,0:T(8,128)(2,1)} %copy-done.5, bf16[128,32,128]{2,1,0:T(8,128)(2,1)} %collective-permute-done.9.refs_1_, bf16[64,256,256]{2,1,0:T(8,128)(2,1)} %copy-done, ...), custom_call_target="tpu_custom_call", output_to_operand_aliasing={{}: (5, {})} | custom-call | flops 7784628224 | bytes 11681792 | tf_op jit(solution)/shard_map/pair_block/pallas_call | solution.py:180
  (12 shorter events, 0.0 us)
Async XLA Ops:
  0.0 84.7 %copy-start.7 = (s32[2]{0:T(128)S(1)}, s32[2]{0:T(128)}, u32[]{:S(2)}) copy-start(s32[2]{0:T(128)} %param.5) | copy-start | bytes 28
  0.0 1.6 copy-start.1
  8.6 110.6 %copy-start.2 = (bf16[128,32,128]{2,1,0:T(8,128)(2,1)}, bf16[128,32,128]{2,1,0:T(8,128)(2,1)S(1)}, u32[]{:S(2)}) copy-start(bf16[128,32,128]{2,1,0:T(8,128)(2,1)S(1)} %whiten.1.refs_0_) | copy-start | bytes 3145732
  8.6 3.0 %collective-permute-start.2 = (bf16[128,32,128]{2,1,0:T(8,128)(2,1)S(1)}, bf16[128,32,128]{2,1,0:T(8,128)(2,1)S(1)}, u32[]{:S(2)}, u32[]{:S(2)}) collective-permute-start(bf16[128,32,128]{2,1,0:T(8,128)(2,1)S(1)} %whiten.1.refs_0_), channel_id=1, source_target_pairs={{0,8},{1,9},{2,10},{3,11},{4,12},{5,13},{6,14},{7,15},{8,0},{9,1},... | collective-permute-start | bytes 3145736 | tf_op jit(solution)/shard_map/ppermute | solution.py:252
  8.7 2.9 %collective-permute-start.3 = (bf16[128,32,128]{2,1,0:T(8,128)(2,1)S(1)}, bf16[128,32,128]{2,1,0:T(8,128)(2,1)}, u32[]{:S(2)}, u32[]{:S(2)}) collective-permute-start(bf16[128,32,128]{2,1,0:T(8,128)(2,1)S(1)} %whiten.1.refs_0_), channel_id=1, source_target_pairs={{0,2},{1,3},{10,12},{11,13},{20,22},{21,23}} | collective-permute-start | bytes 3145736 | tf_op jit(solution)/shard_map/ppermute | solution.py:252
  10.3 25.5 %collective-permute-start = (bf16[128,32,128]{2,1,0:T(8,128)(2,1)S(1)}, bf16[128,32,128]{2,1,0:T(8,128)(2,1)S(1)}, u32[]{:S(2)}, u32[]{:S(2)}) collective-permute-start(bf16[128,32,128]{2,1,0:T(8,128)(2,1)S(1)} %whiten.1.refs_0_), channel_id=1, source_target_pairs={{0,16},{1,17},{2,18},{3,19},{4,20},{5,21},{6,22},{7,23},{8,24},{9,... | collective-permute-start | bytes 3145736 | tf_op jit(solution)/shard_map/ppermute | solution.py:252
  12.9 24.2 %copy-start.3 = (bf16[128,32,128]{2,1,0:T(8,128)(2,1)}, bf16[128,32,128]{2,1,0:T(8,128)(2,1)S(1)}, u32[]{:S(2)}) copy-start(bf16[128,32,128]{2,1,0:T(8,128)(2,1)S(1)} %broadcast_select_fusion.2.refs_0_) | copy-start | bytes 3145732
  12.9 23.0 %collective-permute-start.4 = (bf16[128,32,128]{2,1,0:T(8,128)(2,1)S(1)}, bf16[128,32,128]{2,1,0:T(8,128)(2,1)S(1)}, u32[]{:S(2)}, u32[]{:S(2)}) collective-permute-start(bf16[128,32,128]{2,1,0:T(8,128)(2,1)S(1)} %broadcast_select_fusion.2.refs_0_), channel_id=1, source_target_pairs={{0,2},{1,3},{2,4},{3,5},{10,12},{11,13},{12,14},{13,15},{20,22},{2... | collective-permute-start | bytes 3145736 | tf_op jit(solution)/shard_map/ppermute | solution.py:252
  35.9 8.7 %collective-permute-start.1 = (bf16[128,32,128]{2,1,0:T(8,128)(2,1)S(1)}, bf16[128,32,128]{2,1,0:T(8,128)(2,1)}, u32[]{:S(2)}, u32[]{:S(2)}) collective-permute-start(bf16[128,32,128]{2,1,0:T(8,128)(2,1)S(1)} %collective-permute-done.refs_2_), channel_id=1, source_target_pairs={{0,8},{1,9},{2,10},{3,11},{4,12},{5,13},{6,14},{7,15},{8,0},{9,1},... | collective-permute-start | bytes 3145736 | tf_op jit(solution)/shard_map/ppermute | solution.py:252
  37.1 43.3 %collective-permute-start.5 = (bf16[128,32,128]{2,1,0:T(8,128)(2,1)}, bf16[128,32,128]{2,1,0:T(8,128)(2,1)}, u32[]{:S(2)}, u32[]{:S(2)}) collective-permute-start(bf16[128,32,128]{2,1,0:T(8,128)(2,1)} %broadcast_select_fusion.1.refs_0_), channel_id=1, source_target_pairs={{0,2},{1,3},{2,4},{3,5},{4,6},{5,7},{10,12},{11,13},{12,14},{13,15... | collective-permute-start | bytes 3145736 | tf_op jit(solution)/shard_map/ppermute | solution.py:252
  38.4 72.4 %collective-permute-start.15 = (bf16[128,32,128]{2,1,0:T(8,128)(2,1)S(1)}, bf16[128,32,128]{2,1,0:T(8,128)(2,1)}, u32[]{:S(2)}, u32[]{:S(2)}) collective-permute-start(bf16[128,32,128]{2,1,0:T(8,128)(2,1)S(1)} %whiten.1.refs_0_), channel_id=1, source_target_pairs={{0,1},{1,0},{10,11},{11,10},{20,21},{21,20},{30,31},{31,30}} | collective-permute-start | bytes 3145736 | tf_op jit(solution)/shard_map/ppermute | solution.py:252
  82.7 26.9 %collective-permute-start.6 = (bf16[128,32,128]{2,1,0:T(8,128)(2,1)}, bf16[128,32,128]{2,1,0:T(8,128)(2,1)}, u32[]{:S(2)}, u32[]{:S(2)}) collective-permute-start(bf16[128,32,128]{2,1,0:T(8,128)(2,1)} %broadcast_select_fusion.refs_0_), channel_id=1, source_target_pairs={{0,2},{1,3},{2,4},{3,5},{4,6},{5,7},{10,12},{11,13},{12,14},{13,15... | collective-permute-start | bytes 3145736 | tf_op jit(solution)/shard_map/ppermute | solution.py:252
  87.7 34.6 %collective-permute-start.14 = (bf16[128,32,128]{2,1,0:T(8,128)(2,1)}, bf16[128,32,128]{2,1,0:T(8,128)(2,1)}, u32[]{:S(2)}, u32[]{:S(2)}) collective-permute-start(bf16[128,32,128]{2,1,0:T(8,128)(2,1)} %copy-done.3), channel_id=1, source_target_pairs={{0,1},{1,0},{2,3},{3,2},{10,11},{11,10},{12,13},{13,12},{20,21},{2... | collective-permute-start | bytes 3145736 | tf_op jit(solution)/shard_map/ppermute | solution.py:252
  92.1 44.6 %collective-permute-start.13 = (bf16[128,32,128]{2,1,0:T(8,128)(2,1)}, bf16[128,32,128]{2,1,0:T(8,128)(2,1)}, u32[]{:S(2)}, u32[]{:S(2)}) collective-permute-start(bf16[128,32,128]{2,1,0:T(8,128)(2,1)} %broadcast_select_fusion.1.refs_0_), channel_id=1, source_target_pairs={{0,1},{1,0},{2,3},{3,2},{4,5},{5,4},{10,11},{11,10},{12,13},{13,12... | collective-permute-start | bytes 3145736 | tf_op jit(solution)/shard_map/ppermute | solution.py:252
  100.2 3.3 %copy-start = (bf16[64,256,256]{2,1,0:T(8,128)(2,1)}, bf16[64,256,256]{2,1,0:T(8,128)(2,1)S(1)}, u32[]{:S(2)}) copy-start(bf16[64,256,256]{2,1,0:T(8,128)(2,1)S(1)} %weights.1.refs_2_) | copy-start | bytes 25165828
  109.5 25.9 %collective-permute-start.7 = (bf16[128,32,128]{2,1,0:T(8,128)(2,1)}, bf16[128,32,128]{2,1,0:T(8,128)(2,1)S(1)}, u32[]{:S(2)}, u32[]{:S(2)}) collective-permute-start(bf16[128,32,128]{2,1,0:T(8,128)(2,1)} %collective-permute-done.6.refs_0_), channel_id=1, source_target_pairs={{2,4},{3,5},{4,6},{5,7},{12,14},{13,15}} | collective-permute-start | bytes 3145736 | tf_op jit(solution)/shard_map/ppermute | solution.py:252
  119.8 28.3 %collective-permute-start.12 = (bf16[128,32,128]{2,1,0:T(8,128)(2,1)}, bf16[128,32,128]{2,1,0:T(8,128)(2,1)}, u32[]{:S(2)}, u32[]{:S(2)}) collective-permute-start(bf16[128,32,128]{2,1,0:T(8,128)(2,1)} %broadcast_select_fusion.refs_0_), channel_id=1, source_target_pairs={{0,1},{1,0},{2,3},{3,2},{4,5},{5,4},{6,7},{7,6},{10,11},{11,10},{1... | collective-permute-start | bytes 3145736 | tf_op jit(solution)/shard_map/ppermute | solution.py:252
  123.0 48.5 %collective-permute-start.11 = (bf16[128,32,128]{2,1,0:T(8,128)(2,1)}, bf16[128,32,128]{2,1,0:T(8,128)(2,1)S(1)}, u32[]{:S(2)}, u32[]{:S(2)}) collective-permute-start(bf16[128,32,128]{2,1,0:T(8,128)(2,1)} %collective-permute-done.6.refs_0_), channel_id=1, source_target_pairs={{2,3},{3,2},{4,5},{5,4},{6,7},{7,6},{12,13},{13,12},{14,15},{15,14... | collective-permute-start | bytes 3145736 | tf_op jit(solution)/shard_map/ppermute | solution.py:252
  135.4 2.2 copy-start.4
  135.4 33.7 %collective-permute-start.8 = (bf16[128,32,128]{2,1,0:T(8,128)(2,1)S(1)}, bf16[128,32,128]{2,1,0:T(8,128)(2,1)S(1)}, u32[]{:S(2)}, u32[]{:S(2)}) collective-permute-start(bf16[128,32,128]{2,1,0:T(8,128)(2,1)S(1)} %collective-permute-done.7.refs_0_), channel_id=1, source_target_pairs={{4,6},{5,7}} | collective-permute-start | bytes 3145736 | tf_op jit(solution)/shard_map/ppermute | solution.py:252
  137.6 55.9 %collective-permute-start.10 = (bf16[128,32,128]{2,1,0:T(8,128)(2,1)S(1)}, bf16[128,32,128]{2,1,0:T(8,128)(2,1)}, u32[]{:S(2)}, u32[]{:S(2)}) collective-permute-start(bf16[128,32,128]{2,1,0:T(8,128)(2,1)S(1)} %collective-permute-done.7.refs_0_), channel_id=1, source_target_pairs={{4,5},{5,4},{6,7},{7,6},{14,15},{15,14}} | collective-permute-start | bytes 3145736 | tf_op jit(solution)/shard_map/ppermute | solution.py:252
  169.1 24.4 %copy-start.5 = (bf16[128,32,128]{2,1,0:T(8,128)(2,1)}, bf16[128,32,128]{2,1,0:T(8,128)(2,1)S(1)}, u32[]{:S(2)}) copy-start(bf16[128,32,128]{2,1,0:T(8,128)(2,1)S(1)} %collective-permute-done.8.refs_0_) | copy-start | bytes 3145732
  169.1 45.3 %collective-permute-start.9 = (bf16[128,32,128]{2,1,0:T(8,128)(2,1)S(1)}, bf16[128,32,128]{2,1,0:T(8,128)(2,1)}, u32[]{:S(2)}, u32[]{:S(2)}) collective-permute-start(bf16[128,32,128]{2,1,0:T(8,128)(2,1)S(1)} %collective-permute-done.8.refs_0_), channel_id=1, source_target_pairs={{6,7},{7,6}} | collective-permute-start | bytes 3145736 | tf_op jit(solution)/shard_map/ppermute | solution.py:252
  171.6 1.0 copy-start.6

commit v2 on v1

--- a/solution.py
+++ b/solution.py
@@ -6,6 +6,7 @@
 from jax import lax
 from jax.experimental import pallas as pl
 from jax.experimental.pallas import tpu as pltpu
+from jax.sharding import Mesh
 from jax.sharding import PartitionSpec as P
 
 W = 16
@@ -22,7 +23,7 @@
 
 
 def whiten_kernel(*refs, width, parts):
-    x_refs, out_refs, scratch = refs[:SEGMENTS], refs[SEGMENTS : SEGMENTS + parts], refs[-1]
+    x_refs, whole_ref, out_refs, scratch = refs[:SEGMENTS], refs[SEGMENTS], refs[SEGMENTS + 1 : -1], refs[-1]
 
     def channel(c, carry):
         tiles = [x_ref[pl.ds(c, 2 * W, stride=width), :] for x_ref in x_refs]
@@ -37,21 +38,22 @@
     lax.fori_loop(0, width, channel, 0, unroll=2)
     step = width // parts
     full = scratch[...].reshape(ROWS, width, 128).astype(jnp.bfloat16)
-    for g in range(parts):
-        out_refs[g][...] = full[:, g * step : (g + 1) * step, :]
+    whole_ref[...] = full
+    for g, out_ref in enumerate(out_refs):
+        out_ref[...] = full[:, g * step : (g + 1) * step, :]
 
 
 def whiten(spectra, parts):
     width = spectra.shape[2]
-    step = width // parts
+    widths = [width] + ([width // parts] * parts if parts > 1 else [])
     lines = 2 * W * width
     flat = spectra.reshape(lines, FB)
     return pl.pallas_call(
         functools.partial(whiten_kernel, width=width, parts=parts),
-        out_shape=[jax.ShapeDtypeStruct((ROWS, step, 128), jnp.bfloat16)] * parts,
+        out_shape=[jax.ShapeDtypeStruct((ROWS, n, 128), jnp.bfloat16) for n in widths],
         grid=(1,),
         in_specs=[pl.BlockSpec((lines, ROWS), functools.partial(lambda q, i: (0, q), q)) for q in range(SEGMENTS)],
-        out_specs=[pl.BlockSpec((ROWS, step, 128), lambda i: (0, 0, 0))] * parts,
+        out_specs=[pl.BlockSpec((ROWS, n, 128), lambda i: (0, 0, 0)) for n in widths],
         scratch_shapes=[pltpu.VMEM((ROWS * width, 128), jnp.float32)],
         compiler_params=pltpu.CompilerParams(vmem_limit_bytes=40 << 20),
         name="whiten",
@@ -98,7 +100,7 @@
     )(offsets, *shards)
 
 
-def pair_kernel(meta_ref, *refs, count, step, unroll_sum, unroll_lag):
+def pair_kernel(meta_ref, *refs, count, step, unroll_sum, unroll_lag, pitch):
     x_refs = refs[:count]
     w_ref, t_ref, _, out_ref = refs[count : count + 4]
     xbuf, wide, wbuf, tbuf, cross, lags, stage, sems = refs[count + 4 :]
@@ -151,12 +153,12 @@
             right = jnp.concatenate([real, imag], axis=0)
             out = jnp.dot(tbuf[...], right, preferred_element_type=jnp.float32)
             out = out * (1.0 / math.sqrt(W * FB))
-            lags[pl.ds(2 * h, LAG_PAD, stride=height), :] = out[:, :128]
-            lags[pl.ds(2 * h + 1, LAG_PAD, stride=height), :] = out[:, 128:]
+            lags[pl.ds(2 * h, LAG_PAD, stride=pitch), :] = out[:, :128]
+            lags[pl.ds(2 * h + 1, LAG_PAD, stride=pitch), :] = out[:, 128:]
             return carry
 
         lax.fori_loop(0, height // 2, lag_sums, 0, unroll=unroll_lag)
-        full = lags[...].reshape(LAG_PAD, height, 128)[:LAGS].astype(jnp.bfloat16)
+        full = lags[...].reshape(LAG_PAD, pitch, 128)[:LAGS, :height].astype(jnp.bfloat16)
         stage[...] = full
         backs = [
             pltpu.make_async_copy(
@@ -172,13 +174,13 @@
             back.wait()
 
 
-def pair_block(meta, shards, right, table, out, unroll_sum=2, unroll_lag=2):
+def pair_block(meta, shards, right, table, out, unroll_sum=8, unroll_lag=8, pad=8):
     count = len(shards)
     step = shards[0].shape[1]
     height = count * step
     anywhere = pl.BlockSpec(memory_space=pl.ANY)
     return pl.pallas_call(
-        functools.partial(pair_kernel, count=count, step=step, unroll_sum=unroll_sum, unroll_lag=unroll_lag),
+        functools.partial(pair_kernel, count=count, step=step, unroll_sum=unroll_sum, unroll_lag=unroll_lag, pitch=height+pad),
         out_shape=jax.ShapeDtypeStruct(out.shape, out.dtype),
         grid_spec=pltpu.PrefetchScalarGridSpec(
             num_scalar_prefetch=1,
@@ -191,7 +193,7 @@
                 pltpu.VMEM((PAIRS, 256, 256), jnp.bfloat16),
                 pltpu.VMEM((LAG_PAD, 2 * FB), jnp.bfloat16),
                 pltpu.VMEM((height, FB, 256), jnp.bfloat16),
-                pltpu.VMEM((LAG_PAD * height, 128), jnp.float32),
+                pltpu.VMEM((LAG_PAD * (height + pad), 128), jnp.float32),
                 pltpu.VMEM((LAGS, height, 128), jnp.bfloat16),
                 pltpu.SemaphoreType.DMA((count + 2,)),
             ],
@@ -217,16 +219,80 @@
     return jnp.concatenate([inband * jnp.cos(theta), -inband * jnp.sin(theta)], axis=1).astype(jnp.bfloat16)
 
 
-def bystander_body(whitened, request, table, out):
-    (shard,) = whitened
+def gather_rows(parts, plane_axis, row_axis, side_axis):
+    rows = lax.axis_size(row_axis)
+    sides = lax.axis_size(side_axis)
+    row_id = lax.axis_index(row_axis)
+    side_id = lax.axis_index(side_axis)
+    axes = (row_axis, plane_axis, side_axis)
+    gathered = [lax.all_gather(part, plane_axis, axis=0) for part in parts]
+    out = []
+    for planes in gathered:
+        pieces = [lax.dynamic_index_in_dim(planes, row_id ^ t, 0, keepdims=False) for t in range(rows)]
+        held = []
+        for flip in range(sides):
+            for t in range(rows):
+                piece = pieces[t]
+                if t or flip:
+                    pairs = [
+                        ((r * rows + p) * sides + x, ((r ^ t) * rows + p) * sides + (x ^ flip))
+                        for r in range(rows)
+                        for p in range(rows)
+                        for x in range(sides)
+                        if p >= r ^ t
+                    ]
+                    piece = lax.ppermute(piece, axes, pairs)
+                held.append((piece, row_id ^ t, side_id ^ flip))
+        out.append(held)
+    return out
+
+
+def column_weights(shard, plane_axis, row_axis, side_axis):
+    rows = lax.axis_size(row_axis)
+    row_id = lax.axis_index(row_axis)
     width = shard.shape[1]
-    row_count = lax.axis_size("row")
-    blocks_per_row = lax.axis_size("col") // row_count
+    axes = (row_axis,)
+    own = [shard]
+    for t in range(1, rows):
+        low = t & -t
+        if t == low:
+            own.append(lax.ppermute(shard, axes, [(r, r ^ t) for r in range(rows)]))
+        else:
+            own.append(lax.ppermute(own[t ^ low], axes, [(r, r ^ low) for r in range(rows)]))
+    offsets = jnp.stack([(row_id ^ t) * width for t in range(rows)]).astype(jnp.int32)
+    return weights(offsets, own)
+
+
+def direct_body(spectra, request, table, out):
+    rows = lax.axis_size("row")
+    sides = lax.axis_size("side")
+    width = spectra.shape[2]
+    parts = 2
+    step = width // parts
+    whole, *pieces = whiten(spectra, parts)
+    held = gather_rows(pieces, "plane", "row", "side")
+    right = column_weights(whole, "plane", "row", "side")
+    for g in range(parts):
+        for group in GROUPS:
+            members = [held[g][i] for i in group]
+            places = [(x * rows + r) * width + g * step for _, r, x in members]
+            meta = jnp.stack([request, *places]).astype(jnp.int32)
+            out = pair_block(meta, [m[0] for m in members], right, table, out)
+    return out
+
+
+GROUPS = ((0, 1, 4, 5), (2, 3, 6, 7))
+
+
+def gather_body(spectra, request, table, out):
+    shard = whiten(spectra, 1)[0]
+    width = shard.shape[1]
+    rows = lax.axis_size("row")
+    sides = lax.axis_size("side")
     column = lax.all_gather(shard, "row", axis=1, tiled=True)
-    strided = lax.all_gather(shard, "col", axis=0)
-    grouped = strided.reshape(row_count, blocks_per_row, ROWS, width, 128)
+    grouped = lax.all_gather(shard, ("plane", "side"), axis=0).reshape(rows, sides, ROWS, width, 128)
     moved = lax.all_to_all(grouped, "row", split_axis=0, concat_axis=0)
-    block = jnp.transpose(moved, (2, 1, 0, 3, 4)).reshape(ROWS, blocks_per_row * row_count * width, 128)
+    block = jnp.transpose(moved, (2, 1, 0, 3, 4)).reshape(ROWS, sides * rows * width, 128)
     right = weights(jnp.zeros((1,), jnp.int32), [column])
     group = min(64, block.shape[1])
     for at in range(0, block.shape[1], group):
@@ -235,76 +301,27 @@
     return out
 
 
-def relay_body(whitened, request, table, out, row_count, blocks_per_row):
-    (shard,) = whitened
-    width = shard.shape[1]
-    row_id = lax.axis_index("row")
-    col_id = lax.axis_index("col")
-    plane = col_id // blocks_per_row
-    side = col_id % blocks_per_row
-    depth = plane - row_id
-    devices = [(r, p, x) for r in range(row_count) for p in range(row_count) for x in range(blocks_per_row)]
-
-    def number(r, p, x):
-        return (r * row_count + p) * blocks_per_row + x
-
-    def move(value, pairs):
-        return lax.ppermute(value, ("row", "col"), [(number(*a), number(*b)) for a, b in pairs])
-
-    def core_flip(value):
-        return move(value, [((r, p, x), (r ^ 1, p, x)) for r, p, x in devices])
-
-    def chip_flip(value):
-        return move(value, [((r, p, x), (r ^ 2, p, x)) for r, p, x in devices])
-
-    across = chip_flip(shard)
-    own = [shard, core_flip(shard), across, core_flip(across)]
-    count = len(own)
-    offsets = jnp.stack([(row_id ^ k) * width for k in range(count)])
-    right = weights(offsets, own)
-    came = None
-    for s in range(count + row_count - 1):
-        busy = [(r, p, x) for r, p, x in devices if p >= r and 0 <= s - (p - r) < count]
-        if s == 0:
-            front = own[0]
-        elif s < count:
-            front = jnp.where(depth == 0, own[s], came)
-        else:
-            front = came
-        came = move(front, [((r, p, x), (r, p + 1, x)) for r, p, x in busy if p + 1 < row_count])
-        other = move(front, [((r, p, x), (r, p, 1 - x)) for r, p, x in busy])
-        k = s - depth
-        valid = jnp.where((k >= 0) & (k < count), request, 0)
-        source = row_id ^ jnp.clip(k, 0, count - 1)
-        meta = jnp.stack(
-            [valid, (side * row_count + source) * width, ((1 - side) * row_count + source) * width]
-        ).astype(jnp.int32)
-        out = pair_block(meta, [front, other], right, table, out, 4, 4)
-    return out
-
-
 def body(spectra, pair_mask, band_range):
-    row_id = lax.axis_index("row")
-    col_id = lax.axis_index("col")
-    row_count = lax.axis_size("row")
-    blocks_per_row = lax.axis_size("col") // row_count
+    rows = lax.axis_size("row")
+    sides = lax.axis_size("side")
     width = spectra.shape[2]
-    whitened = whiten(spectra, 1)
-    request = ((pair_mask[0, 0] == 1) & (col_id >= row_id * blocks_per_row)).astype(jnp.int32)
+    request = ((pair_mask[0, 0] == 1) & (lax.axis_index("plane") >= lax.axis_index("row"))).astype(jnp.int32)
     table = make_table(band_range)
-    out = jnp.zeros((LAGS, blocks_per_row * row_count * width, row_count * width), jnp.bfloat16)
-    if row_count == 4 and blocks_per_row == 2:
-        out = relay_body(whitened, request, table, out, row_count, blocks_per_row)
+    out = jnp.zeros((LAGS, sides * rows * width, rows * width), jnp.bfloat16)
+    if (rows, sides) == (4, 2) and width % 32 == 0:
+        out = direct_body(spectra, request, table, out)
     else:
-        out = bystander_body(whitened, request, table, out)
+        out = gather_body(spectra, request, table, out)
     return jnp.transpose(out, (1, 2, 0))
 
 
 def solution(mesh):
+    rows, cols = mesh.devices.shape
+    cut = Mesh(mesh.devices.reshape(rows, rows, cols // rows), ("row", "plane", "side"))
     return jax.shard_map(
         body,
-        mesh=mesh,
-        in_specs=(P(None, None, ("col", "row"), None), P("row", "col"), P()),
-        out_specs=P("row", "col", None),
+        mesh=cut,
+        in_specs=(P(None, None, ("plane", "side", "row"), None), P("row", ("plane", "side")), P()),
+        out_specs=P("row", ("plane", "side"), None),
         check_vma=False,
     )

time: 237 us -> 229 us (0.966)
  waiting for transfers between devices: 81.1 us -> 60.1 us
  Pallas kernels: 99.5 us -> 81.6 us
  starting transfers between devices: 24.5 us -> 40.7 us
  between operations: 1.18 us -> 14.5 us
  local copies, waits for them, and re-layouts: 14.7 us -> 25.6 us
  other arithmetic: 14.5 us -> 5.36 us
    ppermute x16 -> x17, waiting for transfers between devices: 81.1 us -> 28.4 us  [the longest x2 22.1 us: column_weights(): own.append(lax.ppermute(shard, axes, [(r, r ^ t) for r in range(rows)]))]
    all_gather x0 -> x2, waiting for transfers between devices: none -> 31 us  [gather_rows(): gathered = [lax.all_gather(part, plane_axis, axis=0) for part in parts]]
    pallas_call x7 -> x4, Pallas kernels: 86 us -> 67.2 us  [pair_block(): pl.pallas_call(functools.partial(pair_kernel, count=count, step=step, unr...]
    ppermute x16 -> x17, starting transfers between devices: 24.5 us -> 40.6 us  [the longest x14 39 us: gather_rows(): piece = lax.ppermute(piece, axes, pairs)]
    squeeze x0 -> x2, local copies, waits for them, and re-layouts: none -> 5.79 us  [gather_rows(): lax.dynamic_index_in_dim(planes, row_id ^ t, 0, keepdims=False)]
    select_n x3 -> x0, other arithmetic: 4.85 us -> none  [relay_body(): front = jnp.where(depth == 0, own[s], came)]
    another operation x9 -> x2, other arithmetic: 6.43 us -> 2.03 us  [the longest x7 4.4 us: relay_body(): jnp.stack([valid, (side * row_count + source) * width, ((1 - side) * row_...]
    unnamed x16 -> x26, local copies, waits for them, and re-layouts: 5.86 us -> 8.44 us
  transfers between devices with their start and end apart: 16 -> 19, of which waited for: 5 -> 4; matrix products, arithmetic and copies ran while one was open for 10% -> 10% of each run, Pallas kernels for 30% -> 25%
where the time goes in v2:
time: 229 us; the launch traced here: 228 us
  Pallas kernels  81.6 us (36%)
  waiting for transfers between devices  60.1 us (26%)
  starting transfers between devices  40.7 us (18%)
  local copies, waits for them, and re-layouts  25.6 us (11%)
  between operations  14.5 us (6%)
  other arithmetic  5.36 us (2%)
    pallas_call x4, Pallas kernels, pair_block(): pl.pallas_call(functools.partial(pair_kernel, count=count, step=step, unr...  67.2 us
    ppermute x14, starting transfers between devices, gather_rows(): piece = lax.ppermute(piece, axes, pairs)  39 us
    all_gather x2, waiting for transfers between devices, gather_rows(): gathered = [lax.all_gather(part, plane_axis, axis=0) for part in parts]  31 us
    ppermute x2, waiting for transfers between devices, column_weights(): own.append(lax.ppermute(shard, axes, [(r, r ^ t) for r in range(rows)]))  22.1 us
    unnamed x26, local copies, waits for them, and re-layouts  8.44 us
    broadcast_in_dim x1, local copies, waits for them, and re-layouts, body(): out = jnp.zeros((LAGS, sides * rows * width, rows * width), jnp.bfloat16)  8.3 us
    pallas_call x1, Pallas kernels, whiten(): pl.pallas_call(functools.partial(whiten_kernel, width=width, parts=parts)...  7.89 us
    pallas_call x1, Pallas kernels, weights(): pl.pallas_call(functools.partial(weights_kernel, count=count, step=step),...  6.47 us
  transfers between devices with their start and end apart: 19, of which 4 were waited for; matrix products, arithmetic and copies ran while one was open for 10% of the time, Pallas kernels for 25%

profile of v2, /device:TPU:26, one launch (start us, length us, event | category | flops | bytes accessed | tf_op | source)
XLA Modules:
  0.0 227.8 jit_solution(12931705977458021897)
XLA Ops:
  6.5 1.6 copy-done.1
  8.1 7.9 %whiten.1 = (bf16[128,32,128]{2,1,0:T(8,128)(2,1)S(1)}, bf16[128,16,128]{2,1,0:T(8,128)(2,1)}, bf16[128,16,128]{2,1,0:T(8,128)(2,1)}) custom-call(f32[1024,512]{1,0:T(8,128)S(1)} %bitcast.44, f32[1024,512]{1,0:T(8,128)S(1)} %bitcast.45, f32[1024,512]{1,0:T(8,128)S(1)} %bitcast.46, f32[1024,512]{1,0:T(8,128)S(1)} %bitcast.47), custom_call_target="tpu_custom_call" | custom-call | tf_op jit(solution)/shard_map/whiten/pallas_call | solution.py:51
  16.0 0.0 all-gather.7.cloned.1.call-update
  16.1 0.0 all-gather.5.cloned.1.call-start
  16.1 0.7 all-gather.5.cloned.1.call-update
  16.8 1.6 collective-permute-start.5
  18.4 0.0 collective-permute-start.4
  19.1 0.6 stack.110.meta_ref
  19.7 22.1 %collective-permute-done.5.refs_2_ = bf16[128,32,128]{2,1,0:T(8,128)(2,1)S(1)} collective-permute-done((bf16[128,32,128]{2,1,0:T(8,128)(2,1)S(1)}, bf16[128,32,128]{2,1,0:T(8,128)(2,1)S(1)}, u32[]{:S(2)}, u32[]{:S(2)}) %collective-permute-start.5) | collective-permute-done | bytes 1048608 | tf_op jit(solution)/shard_map/ppermute | solution.py:259
  41.8 0.0 collective-permute-start.6
  41.8 0.1 pad_add_fusion.offset_ref
  41.9 0.6 fusion.15
  42.5 1.3 and_convert_fusion
  43.7 1.3 fusion.14
  45.0 15.9 %all-gather.7.cloned.1.call-done = bf16[512,16,128]{2,1,0:T(8,128)(2,1)} async-done(((bf16[128,16,128]{2,1,0:T(8,128)(2,1)}), bf16[512,16,128]{2,1,0:T(8,128)(2,1)}) %all-gather.7.cloned.1.call-update) | async-done | bytes 2097168 | tf_op jit(solution)/shard_map/all_gather | solution.py:228
  60.9 3.0 %dynamic-slice_bitcast_fusion = (bf16[128,16,128]{2,1,0:T(8,128)(2,1)}, bf16[128,16,128]{2,1,0:T(8,128)(2,1)}, bf16[128,16,128]{2,1,0:T(8,128)(2,1)}, bf16[128,16,128]{2,1,0:T(8,128)(2,1)}) fusion(bf16[4,128,16,128]{3,2,1,0:T(8,128)(2,1)} %bitcast.49, s32[]{:T(128)S(6)} %select_n.75, s32[]{:T(128)S(6)} %select_n.74, s32[]{:T(128)S(6)} %select_n.70, ...), kind=kLoop, calls=%fused_computation.1 | loop fusion | bytes 4194320 | tf_op jit(solution)/shard_map/jit(dynamic_index_in_dim)/squeeze | solution.py:231
  63.9 2.0 collective-permute-start.14
  65.8 2.5 %collective-permute-start.16 = (bf16[128,16,128]{2,1,0:T(8,128)(2,1)}, bf16[128,16,128]{2,1,0:T(8,128)(2,1)}, u32[]{:S(2)}, u32[]{:S(2)}) collective-permute-start(bf16[128,16,128]{2,1,0:T(8,128)(2,1)} %get-tuple-element.11), channel_id=1, source_target_pairs={{2,11},{3,10},{4,13},{5,12},{6,15},{7,14},{8,1},{9,0},{10,3},{11,2... | collective-permute-start | bytes 1572872 | tf_op jit(solution)/shard_map/ppermute | solution.py:244
  68.4 3.4 %collective-permute-start.15 = (bf16[128,16,128]{2,1,0:T(8,128)(2,1)}, bf16[128,16,128]{2,1,0:T(8,128)(2,1)}, u32[]{:S(2)}, u32[]{:S(2)}) collective-permute-start(bf16[128,16,128]{2,1,0:T(8,128)(2,1)} %get-tuple-element.12.refs_0_), channel_id=1, source_target_pairs={{0,1},{1,0},{2,3},{3,2},{4,5},{5,4},{6,7},{7,6},{10,11},{11,10},{1... | collective-permute-start | bytes 1572872 | tf_op jit(solution)/shard_map/ppermute | solution.py:244
  71.8 0.6 stack.105.meta_ref
  72.4 0.7 stack.100.meta_ref
  73.1 0.6 stack.90.meta_ref
  73.7 2.0 multiply_convert_fusion.1
  75.6 0.8 pad_maximum_fusion.refs_5_
  76.4 0.0 collective-permute-done.4.refs_1_
  76.4 0.0 collective-permute-done.6.refs_3_
  76.4 6.5 %weights.1.refs_4_ = bf16[64,256,256]{2,1,0:T(8,128)(2,1)S(1)} custom-call(s32[4]{0:T(128)S(1)} %pad_add_fusion.offset_ref, bf16[128,32,128]{2,1,0:T(8,128)(2,1)S(1)} %get-tuple-element.9.refs_0_, bf16[128,32,128]{2,1,0:T(8,128)(2,1)S(1)} %collective-permute-done.4.refs_1_, bf16[128,32,128]{2,1,0:T(8,128)(2,1)S(1)} %collective-permute-done.5.refs_2_, ...), custom_call_target="tpu_custom_call" | custom-call | tf_op jit(solution)/shard_map/weights/pallas_call | solution.py:88
  82.9 3.3 %copy-done = bf16[64,256,256]{2,1,0:T(8,128)(2,1)} copy-done((bf16[64,256,256]{2,1,0:T(8,128)(2,1)}, bf16[64,256,256]{2,1,0:T(8,128)(2,1)S(1)}, u32[]{:S(2)}) %copy-start) | copy-done | bytes 8388632
  86.2 3.4 %collective-permute-start.10 = (bf16[128,16,128]{2,1,0:T(8,128)(2,1)}, bf16[128,16,128]{2,1,0:T(8,128)(2,1)S(1)}, u32[]{:S(2)}, u32[]{:S(2)}) collective-permute-start(bf16[128,16,128]{2,1,0:T(8,128)(2,1)} %get-tuple-element.14), channel_id=1, source_target_pairs={{4,20},{5,21},{6,22},{7,23},{14,30},{15,31},{16,0},{17,1},{18,2},{... | collective-permute-start | bytes 1572872 | tf_op jit(solution)/shard_map/ppermute | solution.py:244
  89.6 2.5 %collective-permute-start.12 = (bf16[128,16,128]{2,1,0:T(8,128)(2,1)}, bf16[128,16,128]{2,1,0:T(8,128)(2,1)S(1)}, u32[]{:S(2)}, u32[]{:S(2)}) collective-permute-start(bf16[128,16,128]{2,1,0:T(8,128)(2,1)} %get-tuple-element.14), channel_id=1, source_target_pairs={{4,21},{5,20},{6,23},{7,22},{14,31},{15,30},{16,1},{17,0},{18,3},{... | collective-permute-start | bytes 1572872 | tf_op jit(solution)/shard_map/ppermute | solution.py:244
  92.1 15.1 %all-gather.5.cloned.1.call-done = bf16[512,16,128]{2,1,0:T(8,128)(2,1)} async-done(((bf16[128,16,128]{2,1,0:T(8,128)(2,1)}), bf16[512,16,128]{2,1,0:T(8,128)(2,1)}) %all-gather.5.cloned.1.call-update) | async-done | bytes 2097168 | tf_op jit(solution)/shard_map/all_gather | solution.py:228
  107.2 2.8 %dynamic-slice_bitcast_fusion.4 = (bf16[128,16,128]{2,1,0:T(8,128)(2,1)}, bf16[128,16,128]{2,1,0:T(8,128)(2,1)S(1)}, bf16[128,16,128]{2,1,0:T(8,128)(2,1)}, bf16[128,16,128]{2,1,0:T(8,128)(2,1)}) fusion(bf16[4,128,16,128]{3,2,1,0:T(8,128)(2,1)} %bitcast.48, s32[]{:T(128)S(6)} %select_n.75, s32[]{:T(128)S(6)} %select_n.74, s32[]{:T(128)S(6)} %select_n.70, ...), kind=kLoop, calls=%fused_computation.5 | loop fusion | bytes 4194320 | tf_op jit(solution)/shard_map/jit(dynamic_index_in_dim)/squeeze | solution.py:231
  110.0 0.0 collective-permute-done.14.refs_1_
  110.0 3.0 %collective-permute-start.11 = (bf16[128,16,128]{2,1,0:T(8,128)(2,1)}, bf16[128,16,128]{2,1,0:T(8,128)(2,1)S(1)}, u32[]{:S(2)}, u32[]{:S(2)}) collective-permute-start(bf16[128,16,128]{2,1,0:T(8,128)(2,1)} %get-tuple-element.13), channel_id=1, source_target_pairs={{6,30},{7,31},{12,20},{13,21},{14,22},{15,23},{18,10},{19,11},{20,... | collective-permute-start | bytes 1572872 | tf_op jit(solution)/shard_map/ppermute | solution.py:244
  113.0 0.0 collective-permute-done.15.refs_2_
  113.0 2.5 %collective-permute-start.13 = (bf16[128,16,128]{2,1,0:T(8,128)(2,1)}, bf16[128,16,128]{2,1,0:T(8,128)(2,1)}, u32[]{:S(2)}, u32[]{:S(2)}) collective-permute-start(bf16[128,16,128]{2,1,0:T(8,128)(2,1)} %get-tuple-element.13), channel_id=1, source_target_pairs={{6,31},{7,30},{12,21},{13,20},{14,23},{15,22},{18,11},{19,10},{20,... | collective-permute-start | bytes 1572872 | tf_op jit(solution)/shard_map/ppermute | solution.py:244
  115.6 0.0 collective-permute-done.16.refs_3_
  115.6 2.0 collective-permute-start.7
  117.6 8.3 %broadcast_in_dim.2.refs_6_ = bf16[201,256,128]{2,1,0:T(8,128)(2,1)} broadcast(bf16[]{:T(256)} %constant.94.clone.1), dimensions={} | broadcast | bytes 13172738 | tf_op jit(solution)/shard_map/broadcast_in_dim | solution.py:310
  125.9 16.7 %pair_block.4.refs_6_ = bf16[201,256,128]{2,1,0:T(8,128)(2,1)} custom-call(s32[5]{0:T(128)} %stack.110.meta_ref, bf16[128,16,128]{2,1,0:T(8,128)(2,1)} %get-tuple-element.12.refs_0_, bf16[128,16,128]{2,1,0:T(8,128)(2,1)} %collective-permute-done.14.refs_1_, bf16[128,16,128]{2,1,0:T(8,128)(2,1)} %collective-permute-done.15.refs_2_, ...), custom_call_target="tpu_custom_call", output_to_operand_aliasing={{}: (7, {})} | custom-call | flops 7784628224 | bytes 11681792 | tf_op jit(solution)/shard_map/pair_block/pallas_call | solution.py:182
  142.6 0.0 collective-permute-done.10.refs_0_
  142.6 1.9 collective-permute-start.9
  144.6 0.0 collective-permute-done.11.refs_1_
  144.6 0.8 copy-done.8
  145.4 3.4 %collective-permute-start = (bf16[128,16,128]{2,1,0:T(8,128)(2,1)}, bf16[128,16,128]{2,1,0:T(8,128)(2,1)S(1)}, u32[]{:S(2)}, u32[]{:S(2)}) collective-permute-start(bf16[128,16,128]{2,1,0:T(8,128)(2,1)} %get-tuple-element.18), channel_id=1, source_target_pairs={{4,20},{5,21},{6,22},{7,23},{14,30},{15,31},{16,0},{17,1},{18,2},{... | collective-permute-start | bytes 1572872 | tf_op jit(solution)/shard_map/ppermute | solution.py:244
  148.8 0.0 collective-permute-done.12.refs_2_
  148.8 3.4 %collective-permute-start.2 = (bf16[128,16,128]{2,1,0:T(8,128)(2,1)}, bf16[128,16,128]{2,1,0:T(8,128)(2,1)S(1)}, u32[]{:S(2)}, u32[]{:S(2)}) collective-permute-start(bf16[128,16,128]{2,1,0:T(8,128)(2,1)} %get-tuple-element.18), channel_id=1, source_target_pairs={{4,21},{5,20},{6,23},{7,22},{14,31},{15,30},{16,1},{17,0},{18,3},{... | collective-permute-start | bytes 1572872 | tf_op jit(solution)/shard_map/ppermute | solution.py:244
  152.2 0.0 collective-permute-done.13.refs_3_
  152.2 2.5 %collective-permute-start.8 = (bf16[128,16,128]{2,1,0:T(8,128)(2,1)S(1)}, bf16[128,16,128]{2,1,0:T(8,128)(2,1)}, u32[]{:S(2)}, u32[]{:S(2)}) collective-permute-start(bf16[128,16,128]{2,1,0:T(8,128)(2,1)S(1)} %get-tuple-element.16.refs_0_), channel_id=1, source_target_pairs={{0,1},{1,0},{2,3},{3,2},{4,5},{5,4},{6,7},{7,6},{10,11},{11,10},{1... | collective-permute-start | bytes 1572872 | tf_op jit(solution)/shard_map/ppermute | solution.py:244
  154.7 16.9 %pair_block.5.refs_6_ = bf16[201,256,128]{2,1,0:T(8,128)(2,1)} custom-call(s32[5]{0:T(128)} %stack.105.meta_ref, bf16[128,16,128]{2,1,0:T(8,128)(2,1)} %copy-done.3, bf16[128,16,128]{2,1,0:T(8,128)(2,1)} %copy-done.8, bf16[128,16,128]{2,1,0:T(8,128)(2,1)} %copy-done.4, ...), custom_call_target="tpu_custom_call", output_to_operand_aliasing={{}: (7, {})} | custom-call | flops 7784628224 | bytes 11681792 | tf_op jit(solution)/shard_map/pair_block/pallas_call | solution.py:182
  171.7 0.0 collective-permute-done.7.refs_1_
  171.7 3.7 %collective-permute-start.1 = (bf16[128,16,128]{2,1,0:T(8,128)(2,1)}, bf16[128,16,128]{2,1,0:T(8,128)(2,1)S(1)}, u32[]{:S(2)}, u32[]{:S(2)}) collective-permute-start(bf16[128,16,128]{2,1,0:T(8,128)(2,1)} %get-tuple-element.17), channel_id=1, source_target_pairs={{6,30},{7,31},{12,20},{13,21},{14,22},{15,23},{18,10},{19,11},{20,... | collective-permute-start | bytes 1572872 | tf_op jit(solution)/shard_map/ppermute | solution.py:244
  175.3 6.2 %collective-permute-done.8.refs_2_ = bf16[128,16,128]{2,1,0:T(8,128)(2,1)} collective-permute-done((bf16[128,16,128]{2,1,0:T(8,128)(2,1)S(1)}, bf16[128,16,128]{2,1,0:T(8,128)(2,1)}, u32[]{:S(2)}, u32[]{:S(2)}) %collective-permute-start.8) | collective-permute-done | bytes 524320 | tf_op jit(solution)/shard_map/ppermute | solution.py:244
  181.6 3.0 %collective-permute-start.3 = (bf16[128,16,128]{2,1,0:T(8,128)(2,1)}, bf16[128,16,128]{2,1,0:T(8,128)(2,1)S(1)}, u32[]{:S(2)}, u32[]{:S(2)}) collective-permute-start(bf16[128,16,128]{2,1,0:T(8,128)(2,1)} %get-tuple-element.17), channel_id=1, source_target_pairs={{6,31},{7,30},{12,21},{13,20},{14,23},{15,22},{18,11},{19,10},{20,... | collective-permute-start | bytes 1572872 | tf_op jit(solution)/shard_map/ppermute | solution.py:244
  184.6 0.8 copy-done.9
  185.4 16.8 %pair_block.6.refs_6_ = bf16[201,256,128]{2,1,0:T(8,128)(2,1)} custom-call(s32[5]{0:T(128)} %stack.100.meta_ref, bf16[128,16,128]{2,1,0:T(8,128)(2,1)} %copy-done.2, bf16[128,16,128]{2,1,0:T(8,128)(2,1)} %copy-done.5, bf16[128,16,128]{2,1,0:T(8,128)(2,1)} %collective-permute-done.8.refs_2_, ...), custom_call_target="tpu_custom_call", output_to_operand_aliasing={{}: (7, {})} | custom-call | flops 7784628224 | bytes 11681792 | tf_op jit(solution)/shard_map/pair_block/pallas_call | solution.py:182
  202.2 0.0 collective-permute-done.refs_0_
  202.3 0.0 collective-permute-done.2.refs_2_
  202.3 0.0 collective-permute-done.3.refs_3_
  202.3 0.7 copy-done.6
  203.0 0.2 copy-done.10
  203.2 0.2 copy-done.7
  203.4 0.8 copy-done.11
  204.2 16.7 %pair_block.7 = bf16[201,256,128]{2,1,0:T(8,128)(2,1)} custom-call(s32[5]{0:T(128)} %stack.90.meta_ref, bf16[128,16,128]{2,1,0:T(8,128)(2,1)} %copy-done.6, bf16[128,16,128]{2,1,0:T(8,128)(2,1)} %copy-done.10, bf16[128,16,128]{2,1,0:T(8,128)(2,1)} %copy-done.7, bf16[128,16,128]{2,1,0:T(8,128)(2,1)} %copy-done.11, ...), custom_call_target="tpu_custom_call", output_to_operand_aliasing={{}: (7, {})} | custom-call | flops 7784628224 | bytes 11681792 | tf_op jit(solution)/shard_map/pair_block/pallas_call | solution.py:182
  (23 shorter events, 0.1 us)
Async XLA Ops:
  6.5 35.3 %copy-start.12 = (s32[2]{0:T(128)S(1)}, s32[2]{0:T(128)}, u32[]{:S(2)}) copy-start(s32[2]{0:T(128)} %param.5) | copy-start | bytes 28
  6.5 54.4 %all-gather.7.cloned.1.call-start = ((), (), s32[]{:S(2)}) async-start(), calls=%async_computation.1 | async-start | bytes 2621440 | tf_op jit(solution)/shard_map/all_gather | solution.py:228
  6.5 1.6 copy-start.1
  16.1 91.1 %all-gather.5.cloned.1.call-start = ((), (), s32[]{:S(2)}) async-start(), calls=%async_computation | async-start | bytes 2621440 | tf_op jit(solution)/shard_map/all_gather | solution.py:228
  16.8 25.0 %collective-permute-start.5 = (bf16[128,32,128]{2,1,0:T(8,128)(2,1)S(1)}, bf16[128,32,128]{2,1,0:T(8,128)(2,1)S(1)}, u32[]{:S(2)}, u32[]{:S(2)}) collective-permute-start(bf16[128,32,128]{2,1,0:T(8,128)(2,1)S(1)} %get-tuple-element.9.refs_0_), channel_id=1, source_target_pairs={{0,16},{8,24},{16,0},{24,8},{1,17},{9,25},{17,1},{25,9},{2,18},{10... | collective-permute-start | bytes 3145736 | tf_op jit(solution)/shard_map/ppermute | solution.py:259
  18.4 58.0 %collective-permute-start.4 = (bf16[128,32,128]{2,1,0:T(8,128)(2,1)S(1)}, bf16[128,32,128]{2,1,0:T(8,128)(2,1)S(1)}, u32[]{:S(2)}, u32[]{:S(2)}) collective-permute-start(bf16[128,32,128]{2,1,0:T(8,128)(2,1)S(1)} %get-tuple-element.9.refs_0_), channel_id=1, source_target_pairs={{0,8},{8,0},{16,24},{24,16},{1,9},{9,1},{17,25},{25,17},{2,10},{10... | collective-permute-start | bytes 3145736 | tf_op jit(solution)/shard_map/ppermute | solution.py:259
  41.8 34.7 %collective-permute-start.6 = (bf16[128,32,128]{2,1,0:T(8,128)(2,1)S(1)}, bf16[128,32,128]{2,1,0:T(8,128)(2,1)}, u32[]{:S(2)}, u32[]{:S(2)}) collective-permute-start(bf16[128,32,128]{2,1,0:T(8,128)(2,1)S(1)} %collective-permute-done.5.refs_2_), channel_id=1, source_target_pairs={{0,8},{8,0},{16,24},{24,16},{1,9},{9,1},{17,25},{25,17},{2,10},{10... | collective-permute-start | bytes 3145736 | tf_op jit(solution)/shard_map/ppermute | solution.py:261
  63.9 46.1 %collective-permute-start.14 = (bf16[128,16,128]{2,1,0:T(8,128)(2,1)}, bf16[128,16,128]{2,1,0:T(8,128)(2,1)}, u32[]{:S(2)}, u32[]{:S(2)}) collective-permute-start(bf16[128,16,128]{2,1,0:T(8,128)(2,1)} %get-tuple-element.11), channel_id=1, source_target_pairs={{2,10},{3,11},{4,12},{5,13},{6,14},{7,15},{8,0},{9,1},{10,2},{11,3... | collective-permute-start | bytes 1572872 | tf_op jit(solution)/shard_map/ppermute | solution.py:244
  65.8 49.7 %collective-permute-start.16 = (bf16[128,16,128]{2,1,0:T(8,128)(2,1)}, bf16[128,16,128]{2,1,0:T(8,128)(2,1)}, u32[]{:S(2)}, u32[]{:S(2)}) collective-permute-start(bf16[128,16,128]{2,1,0:T(8,128)(2,1)} %get-tuple-element.11), channel_id=1, source_target_pairs={{2,11},{3,10},{4,13},{5,12},{6,15},{7,14},{8,1},{9,0},{10,3},{11,2... | collective-permute-start | bytes 1572872 | tf_op jit(solution)/shard_map/ppermute | solution.py:244
  68.4 44.7 %collective-permute-start.15 = (bf16[128,16,128]{2,1,0:T(8,128)(2,1)}, bf16[128,16,128]{2,1,0:T(8,128)(2,1)}, u32[]{:S(2)}, u32[]{:S(2)}) collective-permute-start(bf16[128,16,128]{2,1,0:T(8,128)(2,1)} %get-tuple-element.12.refs_0_), channel_id=1, source_target_pairs={{0,1},{1,0},{2,3},{3,2},{4,5},{5,4},{6,7},{7,6},{10,11},{11,10},{1... | collective-permute-start | bytes 1572872 | tf_op jit(solution)/shard_map/ppermute | solution.py:244
  82.9 3.3 %copy-start = (bf16[64,256,256]{2,1,0:T(8,128)(2,1)}, bf16[64,256,256]{2,1,0:T(8,128)(2,1)S(1)}, u32[]{:S(2)}) copy-start(bf16[64,256,256]{2,1,0:T(8,128)(2,1)S(1)} %weights.1.refs_4_) | copy-start | bytes 25165828
  86.2 56.4 %collective-permute-start.10 = (bf16[128,16,128]{2,1,0:T(8,128)(2,1)}, bf16[128,16,128]{2,1,0:T(8,128)(2,1)S(1)}, u32[]{:S(2)}, u32[]{:S(2)}) collective-permute-start(bf16[128,16,128]{2,1,0:T(8,128)(2,1)} %get-tuple-element.14), channel_id=1, source_target_pairs={{4,20},{5,21},{6,22},{7,23},{14,30},{15,31},{16,0},{17,1},{18,2},{... | collective-permute-start | bytes 1572872 | tf_op jit(solution)/shard_map/ppermute | solution.py:244
  89.6 59.2 %collective-permute-start.12 = (bf16[128,16,128]{2,1,0:T(8,128)(2,1)}, bf16[128,16,128]{2,1,0:T(8,128)(2,1)S(1)}, u32[]{:S(2)}, u32[]{:S(2)}) collective-permute-start(bf16[128,16,128]{2,1,0:T(8,128)(2,1)} %get-tuple-element.14), channel_id=1, source_target_pairs={{4,21},{5,20},{6,23},{7,22},{14,31},{15,30},{16,1},{17,0},{18,3},{... | collective-permute-start | bytes 1572872 | tf_op jit(solution)/shard_map/ppermute | solution.py:244
  110.0 42.2 %copy-start.2 = (bf16[128,16,128]{2,1,0:T(8,128)(2,1)}, bf16[128,16,128]{2,1,0:T(8,128)(2,1)S(1)}, u32[]{:S(2)}) copy-start(bf16[128,16,128]{2,1,0:T(8,128)(2,1)S(1)} %get-tuple-element.16.refs_0_) | copy-start | bytes 1572868
  110.0 34.6 %collective-permute-start.11 = (bf16[128,16,128]{2,1,0:T(8,128)(2,1)}, bf16[128,16,128]{2,1,0:T(8,128)(2,1)S(1)}, u32[]{:S(2)}, u32[]{:S(2)}) collective-permute-start(bf16[128,16,128]{2,1,0:T(8,128)(2,1)} %get-tuple-element.13), channel_id=1, source_target_pairs={{6,30},{7,31},{12,20},{13,21},{14,22},{15,23},{18,10},{19,11},{20,... | collective-permute-start | bytes 1572872 | tf_op jit(solution)/shard_map/ppermute | solution.py:244
  113.0 39.2 %collective-permute-start.13 = (bf16[128,16,128]{2,1,0:T(8,128)(2,1)}, bf16[128,16,128]{2,1,0:T(8,128)(2,1)}, u32[]{:S(2)}, u32[]{:S(2)}) collective-permute-start(bf16[128,16,128]{2,1,0:T(8,128)(2,1)} %get-tuple-element.13), channel_id=1, source_target_pairs={{6,31},{7,30},{12,21},{13,20},{14,23},{15,22},{18,11},{19,10},{20,... | collective-permute-start | bytes 1572872 | tf_op jit(solution)/shard_map/ppermute | solution.py:244
  115.6 56.1 %collective-permute-start.7 = (bf16[128,16,128]{2,1,0:T(8,128)(2,1)}, bf16[128,16,128]{2,1,0:T(8,128)(2,1)S(1)}, u32[]{:S(2)}, u32[]{:S(2)}) collective-permute-start(bf16[128,16,128]{2,1,0:T(8,128)(2,1)} %get-tuple-element.15), channel_id=1, source_target_pairs={{2,10},{3,11},{4,12},{5,13},{6,14},{7,15},{8,0},{9,1},{10,2},{11,3... | collective-permute-start | bytes 1572872 | tf_op jit(solution)/shard_map/ppermute | solution.py:244
  142.6 12.1 %copy-start.3 = (bf16[128,16,128]{2,1,0:T(8,128)(2,1)}, bf16[128,16,128]{2,1,0:T(8,128)(2,1)S(1)}, u32[]{:S(2)}) copy-start(bf16[128,16,128]{2,1,0:T(8,128)(2,1)S(1)} %collective-permute-done.10.refs_0_) | copy-start | bytes 1572868
  142.6 42.0 %collective-permute-start.9 = (bf16[128,16,128]{2,1,0:T(8,128)(2,1)}, bf16[128,16,128]{2,1,0:T(8,128)(2,1)S(1)}, u32[]{:S(2)}, u32[]{:S(2)}) collective-permute-start(bf16[128,16,128]{2,1,0:T(8,128)(2,1)} %get-tuple-element.15), channel_id=1, source_target_pairs={{2,11},{3,10},{4,13},{5,12},{6,15},{7,14},{8,1},{9,0},{10,3},{11,2... | collective-permute-start | bytes 1572872 | tf_op jit(solution)/shard_map/ppermute | solution.py:244
  144.6 0.8 copy-start.8
  145.4 56.8 %collective-permute-start = (bf16[128,16,128]{2,1,0:T(8,128)(2,1)}, bf16[128,16,128]{2,1,0:T(8,128)(2,1)S(1)}, u32[]{:S(2)}, u32[]{:S(2)}) collective-permute-start(bf16[128,16,128]{2,1,0:T(8,128)(2,1)} %get-tuple-element.18), channel_id=1, source_target_pairs={{4,20},{5,21},{6,22},{7,23},{14,30},{15,31},{16,0},{17,1},{18,2},{... | collective-permute-start | bytes 1572872 | tf_op jit(solution)/shard_map/ppermute | solution.py:244
  148.8 6.0 %copy-start.4 = (bf16[128,16,128]{2,1,0:T(8,128)(2,1)}, bf16[128,16,128]{2,1,0:T(8,128)(2,1)S(1)}, u32[]{:S(2)}) copy-start(bf16[128,16,128]{2,1,0:T(8,128)(2,1)S(1)} %collective-permute-done.12.refs_2_) | copy-start | bytes 1572868
  148.8 53.5 %collective-permute-start.2 = (bf16[128,16,128]{2,1,0:T(8,128)(2,1)}, bf16[128,16,128]{2,1,0:T(8,128)(2,1)S(1)}, u32[]{:S(2)}, u32[]{:S(2)}) collective-permute-start(bf16[128,16,128]{2,1,0:T(8,128)(2,1)} %get-tuple-element.18), channel_id=1, source_target_pairs={{4,21},{5,20},{6,23},{7,22},{14,31},{15,30},{16,1},{17,0},{18,3},{... | collective-permute-start | bytes 1572872 | tf_op jit(solution)/shard_map/ppermute | solution.py:244
  152.2 29.3 %collective-permute-start.8 = (bf16[128,16,128]{2,1,0:T(8,128)(2,1)S(1)}, bf16[128,16,128]{2,1,0:T(8,128)(2,1)}, u32[]{:S(2)}, u32[]{:S(2)}) collective-permute-start(bf16[128,16,128]{2,1,0:T(8,128)(2,1)S(1)} %get-tuple-element.16.refs_0_), channel_id=1, source_target_pairs={{0,1},{1,0},{2,3},{3,2},{4,5},{5,4},{6,7},{7,6},{10,11},{11,10},{1... | collective-permute-start | bytes 1572872 | tf_op jit(solution)/shard_map/ppermute | solution.py:244
  171.7 12.9 %copy-start.5 = (bf16[128,16,128]{2,1,0:T(8,128)(2,1)}, bf16[128,16,128]{2,1,0:T(8,128)(2,1)S(1)}, u32[]{:S(2)}) copy-start(bf16[128,16,128]{2,1,0:T(8,128)(2,1)S(1)} %collective-permute-done.7.refs_1_) | copy-start | bytes 1572868
  171.7 30.6 %collective-permute-start.1 = (bf16[128,16,128]{2,1,0:T(8,128)(2,1)}, bf16[128,16,128]{2,1,0:T(8,128)(2,1)S(1)}, u32[]{:S(2)}, u32[]{:S(2)}) collective-permute-start(bf16[128,16,128]{2,1,0:T(8,128)(2,1)} %get-tuple-element.17), channel_id=1, source_target_pairs={{6,30},{7,31},{12,20},{13,21},{14,22},{15,23},{18,10},{19,11},{20,... | collective-permute-start | bytes 1572872 | tf_op jit(solution)/shard_map/ppermute | solution.py:244
  181.6 20.7 %collective-permute-start.3 = (bf16[128,16,128]{2,1,0:T(8,128)(2,1)}, bf16[128,16,128]{2,1,0:T(8,128)(2,1)S(1)}, u32[]{:S(2)}, u32[]{:S(2)}) collective-permute-start(bf16[128,16,128]{2,1,0:T(8,128)(2,1)} %get-tuple-element.17), channel_id=1, source_target_pairs={{6,31},{7,30},{12,21},{13,20},{14,23},{15,22},{18,11},{19,10},{20,... | collective-permute-start | bytes 1572872 | tf_op jit(solution)/shard_map/ppermute | solution.py:244
  184.6 0.8 copy-start.9
  202.2 0.8 copy-start.6
  202.3 1.0 copy-start.10
  202.3 1.1 copy-start.7
  203.4 0.8 copy-start.11
Sparse Core Ops, SparseCore 0:
  16.2 44.6 all-gather.6
  62.5 44.6 all-gather.4
